TPU v7x, 32 devices: a whole 2x2x4 slice. The times are simulated.
32 devices in a mesh: lat: 8 (over z, y), lev: 4 (over x, core).
Axes of the slice: x: 2, y: 2, z: 4, core: 2. Of those that a mesh axis runs over, the one named last changes fastest.
Arguments:
- column_state: bfloat16 [4, 16, 128, 256], P(None, 'lat', 'lev'), may hold values from -6 to 6
- column_target: bfloat16 [4, 16, 128, 256], P(None, 'lat', 'lev'), may hold values from -6 to 6
- member_noise: float32 [2, 16, 128, 256], P(None, 'lat', 'lev'), may hold values from -40 to 40
- land_mask: int32 [16, 256], P('lat'), may hold values 0 or 1
- legendre_basis: float32 [16, 86], P('lat'), may hold values from -0.625 to 0.625
- mode_filter: float32 [86], replicated, may hold values from 0.2 to 2
- weight_in: float32 [384, 256], P('lat', 'lev'), may hold values from -0.3125 to 0.3125
- weight_out: float32 [256, 128], P('lev', 'lat'), may hold values from -0.375 to 0.375
- moment_in: float32 [384, 256], P('lat', 'lev'), may hold values from -0.00012207031 to 0.00012207031
- second_in: float32 [384, 256], P('lat', 'lev'), may hold values from 3.3115596e-10 to 1.3221055e-09
- moment_out: float32 [256, 128], P('lev', 'lat'), may hold values from -0.00024414062 to 0.00024414062
- second_out: float32 [256, 128], P('lev', 'lat'), may hold values from 1.0365769e-09 to 4.138425e-09
Outputs:
- loss_value: float32 [], replicated
- new_weight_in: float32 [384, 256], P('lat', 'lev')
- new_moment_in: float32 [384, 256], P('lat', 'lev')
- new_second_in: float32 [384, 256], P('lat', 'lev')
- new_weight_out: float32 [256, 128], P('lev', 'lat')
- new_moment_out: float32 [256, 128], P('lev', 'lat')
- new_second_out: float32 [256, 128], P('lev', 'lat')
All inputs are finite; a program needn't handle non-finite values. No bound on the sum of `land_mask` on one device may be relied on, other than what follows from the above.
Results may differ from a plain program's by a relative error of at most 0.0046.
Values may be sent and summed in bfloat16 or wider, within the bound.
No kernel may reach another device: no remote copies, remote signals or barrier semaphores. Data moves between devices by JAX's collectives and lax.ppermute only.
A program may use at most 64 MiB of HBM per device.

v0:
```python
import math

import jax
import jax.numpy as jnp
from jax import lax
from jax.sharding import PartitionSpec as P

STEP = 7


NOISE_SCALE = 0.5
LEARN_RATE = 0.02
BETA_ONE = 0.9
BETA_TWO = 0.95
EPSILON = 1e-08
WEIGHT_DECAY = 0.1


def with_halo(shard, sides, width):
    for axis, dim in sides:
        peers, length = (lax.axis_size(axis), shard.shape[dim])
        up = [(i, (i + 1) % peers) for i in range(peers - 1)]
        down = [(j, i) for i, j in up]
        last = lax.slice_in_dim(shard, length - width, length, axis=dim)
        leading = lax.slice_in_dim(shard, 0, width, axis=dim)
        before = lax.ppermute(last, axis, up)
        after = lax.ppermute(leading, axis, down)
        shard = jnp.concatenate([before, shard, after], axis=dim)
    return shard


def spectral(values_in, basis_use, mode_filter):
    blocks, lat_rows, columns = values_in.shape
    flat_cols = jnp.transpose(values_in, (0, 2, 1)).reshape(blocks * columns, lat_rows)
    coefficients = lax.psum_scatter(
        jnp.dot(flat_cols, basis_use, preferred_element_type=jnp.float32),
        "lat",
        scatter_dimension=0,
        tiled=True,
    )
    filtered = (mode_filter[None, :] * coefficients).astype(jnp.bfloat16)
    returned = lax.dot_general(
        lax.all_gather(filtered, "lat", axis=0, tiled=True),
        basis_use,
        (((1,), (1,)), ((), ())),
        preferred_element_type=jnp.float32,
    )
    return jnp.transpose(returned.reshape(blocks, columns, lat_rows), (0, 2, 1))


def adamw(weight, moment_one, moment_two, gradient):
    moment_one = BETA_ONE * moment_one + (1.0 - BETA_ONE) * gradient
    moment_two = BETA_TWO * moment_two + (1.0 - BETA_TWO) * gradient * gradient
    fix_one = 1.0 - BETA_ONE**STEP
    fix_two = 1.0 - BETA_TWO**STEP
    update = moment_one / fix_one / (jnp.sqrt(moment_two / fix_two) + EPSILON)
    return (weight - LEARN_RATE * (update + WEIGHT_DECAY * weight), moment_one, moment_two)


def body(
    column_state,
    column_target,
    member_noise,
    land_mask,
    legendre_basis,
    mode_filter,
    weight_in,
    weight_out,
    moment_in,
    second_in,
    moment_out,
    second_out,
):
    item_count, lat_rows, local_feats, longitudes = column_state.shape
    members = member_noise.shape[0]
    lat_total = lax.axis_size("lat") * lat_rows
    all_feats = local_feats * lax.axis_size("lev")
    full_in, full_out = (
        lax.all_gather(weight_in.astype(jnp.bfloat16), "lat", axis=0, tiled=True),
        lax.all_gather(weight_out.astype(jnp.bfloat16), "lat", axis=1, tiled=True),
    )
    row_index = (lax.axis_index("lat") * lat_rows + jnp.arange(lat_rows, dtype=jnp.int32)).astype(
        jnp.float32
    )
    cosine = jnp.cos((row_index + 0.5) * (math.pi / lat_total) - 0.5 * math.pi)
    cell_weight = cosine[:, None] * land_mask.astype(jnp.float32)
    power_local = jnp.sum(member_noise * member_noise, axis=(1, 3))
    power_sum, weight_sum = lax.psum((power_local, jnp.sum(cell_weight)), "lat")
    power = power_sum / (lat_total * longitudes)
    scaled = member_noise * lax.rsqrt(power + 1e-05)[:, None, :, None]
    state_full = column_state.astype(jnp.float32)
    target_full = column_target.astype(jnp.float32)
    inputs = (state_full[:, None] + NOISE_SCALE * scaled[None]).astype(jnp.bfloat16)
    use_in, use_out = (full_in, full_out)
    gathered = lax.all_gather(inputs, "lev", axis=3, tiled=True)
    padded = with_halo(gathered, (("lat", 2),), 1)
    stacked = jnp.concatenate(
        [padded[:, :, 0:lat_rows], padded[:, :, 1 : lat_rows + 1], padded[:, :, 2 : lat_rows + 2]],
        axis=3,
    )
    pre_act = jnp.einsum("imncl,ch->imnlh", stacked, use_in, preferred_element_type=jnp.float32)
    hidden = jax.nn.silu(pre_act).astype(jnp.bfloat16)
    partial_out = jnp.einsum("imnlh,hf->imnfl", hidden, use_out, preferred_element_type=jnp.float32)
    branch = lax.psum_scatter(partial_out, "lev", scatter_dimension=3, tiled=True).astype(
        jnp.bfloat16
    )
    basis_use = legendre_basis.astype(jnp.bfloat16)
    field_shape = (item_count * members, lat_rows, local_feats * longitudes)
    tendency = spectral(branch.reshape(field_shape), basis_use, mode_filter)
    prediction = state_full[:, None] + tendency.reshape(
        item_count, members, lat_rows, local_feats, longitudes
    )
    d_one = prediction[:, 0] - target_full
    d_two = prediction[:, 1] - target_full
    normaliser = item_count * all_feats * weight_sum
    error_cell = 0.375 * (d_one * d_one + d_two * d_two) + 0.25 * d_one * d_two
    loss_value = lax.psum(
        jnp.sum(cell_weight[None, :, None, :] * error_cell) / normaliser, ("lat", "lev")
    )
    cell_scale = cell_weight[None, :, None, :] / normaliser
    g_one = cell_scale * (0.75 * d_one + 0.25 * d_two)
    g_two = cell_scale * (0.75 * d_two + 0.25 * d_one)
    g_pred = jnp.stack([g_one, g_two], axis=1).astype(jnp.bfloat16).reshape(field_shape)
    g_branch = spectral(g_pred, basis_use, mode_filter).astype(jnp.bfloat16)
    g_branch = g_branch.reshape(item_count, members, lat_rows, local_feats, longitudes)
    g_whole = lax.all_gather(g_branch, "lev", axis=3, tiled=True)
    g_hidden = jnp.einsum("imnfl,hf->imnlh", g_whole, use_out, preferred_element_type=jnp.float32)
    sigmoid_z = jax.nn.sigmoid(pre_act)
    g_pre = (g_hidden * sigmoid_z * (1.0 + pre_act * (1.0 - sigmoid_z))).astype(jnp.bfloat16)
    grad_in = jnp.einsum("imncl,imnlh->ch", stacked, g_pre, preferred_element_type=jnp.float32)
    grad_out = jnp.einsum("imnlh,imnfl->hf", hidden, g_whole, preferred_element_type=jnp.float32)
    reduced_in, reduced_out = (
        lax.psum_scatter(grad_in, "lat", scatter_dimension=0, tiled=True),
        lax.psum_scatter(grad_out, "lat", scatter_dimension=1, tiled=True),
    )
    new_weight_in, new_moment_in, new_second_in = adamw(weight_in, moment_in, second_in, reduced_in)
    new_weight_out, new_moment_out, new_second_out = adamw(
        weight_out, moment_out, second_out, reduced_out
    )
    return (
        loss_value,
        new_weight_in,
        new_moment_in,
        new_second_in,
        new_weight_out,
        new_moment_out,
        new_second_out,
    )


def solution(mesh):
    return jax.shard_map(
        body,
        mesh=mesh,
        in_specs=(
            P(None, "lat", "lev", None),
            P(None, "lat", "lev", None),
            P(None, "lat", "lev", None),
            P("lat", None),
            P("lat", None),
            P(),
            P("lat", "lev"),
            P("lev", "lat"),
            P("lat", "lev"),
            P("lat", "lev"),
            P("lev", "lat"),
            P("lev", "lat"),
        ),
        out_specs=(
            P(),
            P("lat", "lev"),
            P("lat", "lev"),
            P("lat", "lev"),
            P("lev", "lat"),
            P("lev", "lat"),
            P("lev", "lat"),
        ),
        check_vma=False,
    )
```

profile of v0, /device:TPU:0, one launch (start us, length us, event | category | flops | bytes accessed | tf_op | source)
XLA Modules:
  0.0 1468.1 jit_solution(7338895997117777641)
XLA Ops:
  7.3 1.0 multiply_reduce_fusion.1
  8.3 1.4 fusion.19
  9.6 23.8 %all-reduce.1 = (f32[2,32]{1,0:T(2,128)S(1)}, f32[]{:T(128)}) all-reduce(f32[2,32]{1,0:T(2,128)S(1)} %multiply_reduce_fusion.1, f32[]{:T(128)} %get-tuple-element.15), channel_id=1, replica_groups=mesh['lat'=8,'lev'=4] {'lat'}, use_global_device_ids=true, to_apply=%region_1.0 | all-reduce | flops 65 | bytes 520 | tf_op jit(solution)/shard_map/psum | solution.py:88
  33.4 1.0 multiply_multiply_fusion
  34.4 0.9 convert_element_type.59
  35.3 0.7 add_convert_fusion
  36.1 14.1 all-gather.5.cloned.1.call-done
  50.2 1.3 fusion.20
  51.5 3.4 collective-permute-start
  54.9 1.3 collective-permute-start.1
  56.2 0.7 convert_element_type.61
  56.9 0.7 convert_element_type.63
  57.6 1.2 dynamic-slice
  59.5 0.7 convert_element_type.65
  60.2 43.3 %all_gather.20 = bf16[64,128]{0,1:T(8,128)(2,1)S(1)} all-gather(bf16[64,16]{0,1:T(8,128)(2,1)S(1)} %convert_element_type.63), channel_id=1, replica_groups=mesh['lat'=8,'lev'=4] {'lat'}, dimensions={1}, use_global_device_ids=true | all-gather | bytes 18432 | tf_op jit(solution)/shard_map/all_gather | solution.py:80
  103.5 30.5 %all_gather.19 = bf16[384,64]{1,0:T(8,128)(2,1)S(1)} all-gather(bf16[48,64]{1,0:T(8,128)(2,1)S(1)} %convert_element_type.61), channel_id=1, replica_groups=mesh['lat'=8,'lev'=4] {'lat'}, dimensions={0}, use_global_device_ids=true | all-gather | bytes 55296 | tf_op jit(solution)/shard_map/all_gather | solution.py:79
  134.0 2.5 fusion.4
  136.5 1.0 copy-done.13
  137.5 1.9 convolution_bitcast_fusion
  139.4 2.4 copy.27
  141.8 40.6 %all-reduce.3 = bf16[4,2,2,128,256]{4,0,2,1,3:T(4,128)(2,1)S(1)} all-reduce(f32[4,2,2,128,256]{4,0,2,1,3:T(4,128)S(1)} %copy.27), channel_id=2, replica_groups=mesh['lat'=8,'lev'=4] {'lev'}, use_global_device_ids=true, to_apply=%region_2.0.clone | all-reduce | flops 524288 | bytes 3145728
  182.4 0.1 dynamic-slice_convert_fusion
  182.6 0.1 reshape.54
  182.7 0.3 copy.39
  183.0 9.4 fusion.21
  192.4 370.2 %reduce-scatter.5.cloned.1.call-done = f32[8192,86]{0,1:T(8,128)} async-done(((f32[65536,86]{0,1:T(8,128)}), f32[8192,86]{0,1:T(8,128)}) %reduce-scatter.5.cloned.1.call-update) | async-done | bytes 2818064 | tf_op jit(solution)/shard_map/reduce_scatter | solution.py:35
  562.6 3.3 multiply_convert_fusion.1
  566.6 161.9 %all-gather.7.cloned.1.call-done = bf16[65536,86]{0,1:T(8,128)(2,1)} async-done(((bf16[8192,86]{0,1:T(8,128)(2,1)}), bf16[65536,86]{0,1:T(8,128)(2,1)}) %all-gather.7.cloned.1.call-update) | async-done | bytes 11272208 | tf_op jit(solution)/shard_map/all_gather | solution.py:43
  728.5 5.9 fusion.22
  734.4 0.5 reshape.57
  735.0 0.8 fusion.6
  735.8 0.1 convert_element_type.68
  735.9 0.3 copy.40
  736.2 9.4 fusion.23
  745.7 372.0 %reduce-scatter.7.cloned.1.call-done = f32[8192,86]{0,1:T(8,128)} async-done(((f32[65536,86]{0,1:T(8,128)}), f32[8192,86]{0,1:T(8,128)}) %reduce-scatter.7.cloned.1.call-update) | async-done | bytes 2818064 | tf_op jit(solution)/shard_map/reduce_scatter | solution.py:35
  1117.7 3.3 multiply_convert_fusion
  1121.0 162.6 %all-gather.9.cloned.1.call-done = bf16[65536,86]{0,1:T(8,128)(2,1)} async-done(((bf16[8192,86]{0,1:T(8,128)(2,1)}), bf16[65536,86]{0,1:T(8,128)(2,1)}) %all-gather.9.cloned.1.call-update) | async-done | bytes 11272208 | tf_op jit(solution)/shard_map/all_gather | solution.py:43
  1283.6 5.9 convolution_convert_fusion
  1289.5 0.2 copy.45
  1289.7 0.8 copy.44
  1290.5 0.2 reduce-scatter.11.cloned.1.call-start
  1291.4 38.6 %psum.23 = f32[]{:T(128)} all-reduce(f32[]{:T(128)S(6)} %div.54), channel_id=1, replica_groups=mesh['lat'=8,'lev'=4] {'lat','lev'}, use_global_device_ids=true, to_apply=%region_7.8 | all-reduce | flops 1 | bytes 8 | tf_op jit(solution)/shard_map/psum | solution.py:117
  1330.0 2.3 convolution_bitcast_fusion.2
  1332.5 3.4 convolution_bitcast_fusion.1
  1335.8 59.8 %reduce-scatter.11.cloned.1.call-done = f32[64,16]{0,1:T(8,128)} async-done(((f32[64,128]{0,1:T(8,128)}), f32[64,16]{0,1:T(8,128)}) %reduce-scatter.11.cloned.1.call-update) | async-done | bytes 4112 | tf_op jit(solution)/shard_map/reduce_scatter | solution.py:134
  1395.7 1.3 multiply_subtract_fusion.1
  1397.0 62.9 %reduce-scatter.9.cloned.1.call-done = f32[48,64]{1,0:T(8,128)} async-done(((f32[384,64]{1,0:T(8,128)}), f32[48,64]{1,0:T(8,128)}) %reduce-scatter.9.cloned.1.call-update) | async-done | bytes 12304 | tf_op jit(solution)/shard_map/reduce_scatter | solution.py:133
  1459.9 1.4 multiply_subtract_fusion
  (54 shorter events, 0.7 us)
Async XLA Ops:
  7.2 43.0 %all-gather.5.cloned.1.call-start = ((), (), s32[]{:S(2)}) async-start(), calls=%async_computation.4 | async-start | bytes 1310720 | tf_op jit(solution)/shard_map/all_gather | solution.py:95
  36.1 526.5 %reduce-scatter.5.cloned.1.call-start = ((), (), s32[]{:S(2)}) async-start(), calls=%async_computation.5 | async-start | bytes 25952256 | tf_op jit(solution)/shard_map/reduce_scatter | solution.py:35
  51.5 82.6 %collective-permute-start = (bf16[4,2,1,128,256]{4,3,2,1,0:T(8,128)(2,1)S(1)}, bf16[4,2,1,128,256]{4,3,2,1,0:T(8,128)(2,1)S(1)}, u32[]{:S(2)}, u32[]{:S(2)}) collective-permute-start(bf16[4,2,1,128,256]{4,3,2,1,0:T(8,128)(2,1)S(1)} %get-tuple-element.17), channel_id=1, source_target_pairs={{0,4},{4,8},{8,12},{12,16},{16,20},{20,24},{24,28},{1,5},{5,9},{9,... | collective-permute-start | bytes 1572872 | tf_op jit(solution)/shard_map/ppermute | solution.py:26
  54.9 79.1 %collective-permute-start.1 = (bf16[4,2,1,128,256]{4,3,2,1,0:T(8,128)(2,1)S(1)}, bf16[4,2,1,128,256]{4,3,2,1,0:T(8,128)(2,1)S(1)}, u32[]{:S(2)}, u32[]{:S(2)}) collective-permute-start(bf16[4,2,1,128,256]{4,3,2,1,0:T(8,128)(2,1)S(1)} %get-tuple-element.18), channel_id=1, source_target_pairs={{4,0},{8,4},{12,8},{16,12},{20,16},{24,20},{28,24},{5,1},{9,5},{13... | collective-permute-start | bytes 1572872 | tf_op jit(solution)/shard_map/ppermute | solution.py:27
  134.0 2.5 copy-start.9
  134.0 2.5 copy-start.11
  136.5 1.0 copy-start.13
  192.4 370.3 %copy-start.8 = (f32[86]{0:T(128)S(1)}, f32[86]{0:T(128)}, u32[]{:S(2)}) copy-start(f32[86]{0:T(128)} %param.17) | copy-start | bytes 1036
  192.4 536.1 %all-gather.7.cloned.1.call-start = ((), (), s32[]{:S(2)}) async-start(), calls=%async_computation.6 | async-start | bytes 12976128 | tf_op jit(solution)/shard_map/all_gather | solution.py:43
  565.9 551.8 %reduce-scatter.7.cloned.1.call-start = ((), (), s32[]{:S(2)}) async-start(), calls=%async_computation.7 | async-start | bytes 25952256 | tf_op jit(solution)/shard_map/reduce_scatter | solution.py:35
  566.6 168.4 %copy-start.1 = (bf16[4,2,32,256]{3,2,1,0:T(8,128)(2,1)S(1)}, bf16[4,2,32,256]{3,2,1,0:T(8,128)(2,1)}, u32[]{:S(2)}) copy-start(bf16[4,2,32,256]{3,2,1,0:T(8,128)(2,1)} %param.13) | copy-start | bytes 393220
  745.6 537.9 %all-gather.9.cloned.1.call-start = ((), (), s32[]{:S(2)}) async-start(), calls=%async_computation.8 | async-start | bytes 12976128 | tf_op jit(solution)/shard_map/all_gather | solution.py:43
  1120.9 209.0 %copy-start.14 = (f32[4,2,2,256,64]{3,4,2,1,0:T(8,128)S(1)}, f32[4,2,2,256,64]{3,4,2,1,0:T(8,128)}, u32[]{:S(2)}) copy-start(f32[4,2,2,256,64]{3,4,2,1,0:T(8,128)} %copy-done.13) | copy-start | bytes 3145732
  1120.9 209.0 %all-gather.11.cloned.1.call-start = ((), (), s32[]{:S(2)}) async-start(), calls=%async_computation.9 | async-start | bytes 1310720 | tf_op jit(solution)/shard_map/all_gather | solution.py:126
  1289.5 42.9 %copy-start = (bf16[4,2,2,128,256]{4,3,2,1,0:T(8,128)(2,1)S(1)}, bf16[4,2,2,128,256]{4,3,2,1,0:T(8,128)(2,1)}, u32[]{:S(2)}) copy-start(bf16[4,2,2,128,256]{4,3,2,1,0:T(8,128)(2,1)} %all-gather.5.cloned.1.call-done) | copy-start | bytes 3145732
  1289.5 42.9 %copy-start.10 = (bf16[4,2,1,128,256]{4,3,2,1,0:T(8,128)(2,1)S(1)}, bf16[4,2,1,128,256]{4,3,2,1,0:T(8,128)(2,1)}, u32[]{:S(2)}) copy-start(bf16[4,2,1,128,256]{4,3,2,1,0:T(8,128)(2,1)} %copy-done.9) | copy-start | bytes 1572868
  1289.5 42.9 %copy-start.12 = (bf16[4,2,1,128,256]{4,3,2,1,0:T(8,128)(2,1)S(1)}, bf16[4,2,1,128,256]{4,3,2,1,0:T(8,128)(2,1)}, u32[]{:S(2)}) copy-start(bf16[4,2,1,128,256]{4,3,2,1,0:T(8,128)(2,1)} %copy-done.11) | copy-start | bytes 1572868
  1290.5 105.2 %reduce-scatter.11.cloned.1.call-start = ((), (), s32[]{:S(2)}) async-start(), calls=%async_computation.11 | async-start | bytes 73728 | tf_op jit(solution)/shard_map/reduce_scatter | solution.py:134
  1332.3 63.4 %copy-start.3 = (f32[64,16]{0,1:T(8,128)S(1)}, f32[64,16]{0,1:T(8,128)}, u32[]{:S(2)}) copy-start(f32[64,16]{0,1:T(8,128)} %param.19) | copy-start | bytes 12292
  1332.3 63.3 %copy-start.6 = (f32[64,16]{0,1:T(8,128)S(1)}, f32[64,16]{0,1:T(8,128)}, u32[]{:S(2)}) copy-start(f32[64,16]{0,1:T(8,128)} %param.22) | copy-start | bytes 12292
  1332.3 63.3 %copy-start.7 = (f32[64,16]{0,1:T(8,128)S(1)}, f32[64,16]{0,1:T(8,128)}, u32[]{:S(2)}) copy-start(f32[64,16]{0,1:T(8,128)} %param.23) | copy-start | bytes 12292
  1332.3 127.6 %copy-start.2 = (f32[48,64]{1,0:T(8,128)S(1)}, f32[48,64]{1,0:T(8,128)}, u32[]{:S(2)}) copy-start(f32[48,64]{1,0:T(8,128)} %param.18) | copy-start | bytes 36868
  1332.4 127.6 %copy-start.4 = (f32[48,64]{1,0:T(8,128)S(1)}, f32[48,64]{1,0:T(8,128)}, u32[]{:S(2)}) copy-start(f32[48,64]{1,0:T(8,128)} %param.20) | copy-start | bytes 36868
  1332.4 127.6 %copy-start.5 = (f32[48,64]{1,0:T(8,128)S(1)}, f32[48,64]{1,0:T(8,128)}, u32[]{:S(2)}) copy-start(f32[48,64]{1,0:T(8,128)} %param.21) | copy-start | bytes 36868
  1332.4 127.5 %reduce-scatter.9.cloned.1.call-start = ((), (), s32[]{:S(2)}) async-start(), calls=%async_computation.10 | async-start | bytes 221184 | tf_op jit(solution)/shard_map/reduce_scatter | solution.py:133
Sparse Core Ops, SparseCore 0:
  36.2 13.9 all-gather.4
  192.5 370.0 reduce-scatter.4
  566.0 162.4 all-gather.6
  745.7 371.8 reduce-scatter.6
  1121.1 162.4 all-gather.8
  1290.6 15.3 all-gather.10
  1332.4 63.1 reduce-scatter.10
  1398.9 60.9 reduce-scatter.8
where the time goes:
time: 1470 us
  waiting for transfers between devices  1200 us (82%)
  blocking collectives  177 us (12%)
  matrix products  40.6 us (3%)
  other arithmetic  17.3 us (1%)
  between operations  16.4 us (1%)
    reduce_scatter x2, waiting for transfers between devices, spectral(): lax.psum_scatter(jnp.dot(flat_cols, basis_use, preferred_element_type=jnp...  742 us
    all_gather x2, waiting for transfers between devices, spectral(): lax.all_gather(filtered, 'lat', axis=0, tiled=True)  324 us
    reduce_scatter x1, waiting for transfers between devices, body(): lax.psum_scatter(grad_in, 'lat', scatter_dimension=0, tiled=True)  62.9 us
    reduce_scatter x1, waiting for transfers between devices, body(): lax.psum_scatter(grad_out, 'lat', scatter_dimension=1, tiled=True)  59.8 us
    all_gather x1, blocking collectives, body(): lax.all_gather(weight_out.astype(jnp.bfloat16), 'lat', axis=1, tiled=True)  43.3 us
    unnamed x1, blocking collectives  40.6 us
    psum x1, blocking collectives, body(): lax.psum(jnp.sum(cell_weight[None, :, None, :] * error_cell) / normaliser...  38.6 us
    all_gather x1, blocking collectives, body(): lax.all_gather(weight_in.astype(jnp.bfloat16), 'lat', axis=0, tiled=True)  30.5 us
  transfers between devices with their start and end apart: 10, of which 7 were waited for; matrix products, arithmetic and copies ran while one was open for 1% of the time, Pallas kernels for 0%

commit v1 on v0

v1 whole, which is shorter than its diff:
```python
import math

import jax
import jax.numpy as jnp
from jax import lax
from jax.sharding import PartitionSpec as P

STEP = 7
NOISE_SCALE = 0.5
LEARN_RATE = 0.02
BETA_ONE = 0.9
BETA_TWO = 0.95
EPSILON = 1e-08
WEIGHT_DECAY = 0.1
EVERY = ("lat", "lev")
BF = jnp.bfloat16
F32 = jnp.float32


def adamw(weight, moment_one, moment_two, gradient):
    moment_one = BETA_ONE * moment_one + (1.0 - BETA_ONE) * gradient
    moment_two = BETA_TWO * moment_two + (1.0 - BETA_TWO) * gradient * gradient
    fix_one = 1.0 - BETA_ONE**STEP
    fix_two = 1.0 - BETA_TWO**STEP
    update = moment_one / fix_one / (jnp.sqrt(moment_two / fix_two) + EPSILON)
    return (weight - LEARN_RATE * (update + WEIGHT_DECAY * weight), moment_one, moment_two)


def parts_of(value, count):
    terms = []
    for _ in range(count):
        term = value.astype(BF)
        terms.append(term)
        value = value - lax.optimization_barrier(term).astype(F32)
    return terms


def exchange(pieces, devices):
    flat = jnp.concatenate([p.reshape(devices, -1) for p in pieces], axis=1)
    size = flat.shape[1]
    flat = jnp.pad(flat, ((0, 0), (0, -size % 1024)))
    flat = lax.all_to_all(flat.reshape(devices, -1, 128), EVERY, 0, 0, tiled=True).reshape(devices, -1)
    out, start = [], 0
    for p in pieces:
        count = math.prod(p.shape[1:])
        out.append(lax.slice_in_dim(flat, start, start + count, axis=1).reshape(p.shape))
        start += count
    return out


def body(
    column_state,
    column_target,
    member_noise,
    land_mask,
    legendre_basis,
    mode_filter,
    weight_in,
    weight_out,
    moment_in,
    second_in,
    moment_out,
    second_out,
):
    items, rows, feats, lons = column_state.shape
    members = member_noise.shape[0]
    lats, levs = lax.axis_size("lat"), lax.axis_size("lev")
    devices = lats * levs
    lat_total, all_feats, own = lats * rows, levs * feats, lons // devices
    modes = legendre_basis.shape[1]

    def cut(field):
        field = jnp.moveaxis(field.astype(BF), -1, 0)
        return field.reshape((devices, own) + field.shape[1:])

    def every(value):
        return jnp.broadcast_to(value[None], (devices,) + value.shape)

    def whole(field):
        field = field.reshape(lats, levs, own, -1, rows, feats)
        return field.transpose(3, 0, 4, 2, 1, 5).reshape(-1, lat_total, own, all_feats)

    squares = jnp.sum(member_noise * member_noise, axis=(1, 3))
    mask_count = jnp.sum(land_mask, axis=1).astype(F32)
    got = exchange(
        [
            cut(column_state),
            cut(column_target),
            cut(member_noise),
            cut(land_mask),
            *[every(s) for s in parts_of(squares, 3)],
            every(mask_count.astype(BF)),
            every(legendre_basis.astype(BF)),
            every(weight_in.astype(BF)),
            every(weight_out.astype(BF)),
        ],
        devices,
    )
    state = whole(got[0]).astype(F32)
    target = whole(got[1]).astype(F32)
    noise = whole(got[2]).astype(F32)
    mask = got[3].reshape(lats, levs, own, rows)[:, 0].transpose(0, 2, 1).reshape(lat_total, own).astype(F32)
    squares = sum(g.astype(F32) for g in got[4:7]).reshape(lats, levs, members, feats).sum(0)
    power = squares.transpose(1, 0, 2).reshape(members, all_feats) / (lat_total * lons)
    counts = got[7].reshape(lats, levs, rows)[:, 0].reshape(lat_total).astype(F32)
    basis = got[8].reshape(lats, levs, rows, modes)[:, 0].reshape(lat_total, modes)
    full_in = got[9].reshape(lats, levs, *weight_in.shape).transpose(0, 2, 1, 3).reshape(3 * all_feats, -1)
    full_out = got[10].reshape(lats, levs, *weight_out.shape).transpose(1, 2, 0, 3).reshape(-1, all_feats)

    cosine = jnp.cos((jnp.arange(lat_total, dtype=F32) + 0.5) * (math.pi / lat_total) - 0.5 * math.pi)
    cell_weight = cosine[:, None] * mask
    normaliser = items * all_feats * jnp.sum(cosine * counts)

    scaled = noise * lax.rsqrt(power + 1e-05)[:, None, None, :]
    inputs = (state[:, None] + NOISE_SCALE * scaled[None]).astype(BF)
    padded = jnp.pad(inputs, ((0, 0), (0, 0), (1, 1), (0, 0), (0, 0)))
    stacked = jnp.concatenate([padded[:, :, t : t + lat_total] for t in range(3)], axis=-1)

    def spectral(field):
        coefficients = jnp.einsum("nk,imnlf->imklf", basis, field, preferred_element_type=F32)
        filtered = (mode_filter[:, None, None] * coefficients).astype(BF)
        return jnp.einsum("nk,imklf->imnlf", basis, filtered, preferred_element_type=F32)

    pre_act = jnp.einsum("imnlc,ch->imnlh", stacked, full_in, preferred_element_type=F32)
    hidden = jax.nn.silu(pre_act).astype(BF)
    branch = jnp.einsum("imnlh,hf->imnlf", hidden, full_out, preferred_element_type=F32).astype(BF)
    prediction = state[:, None] + spectral(branch)
    d_one = prediction[:, 0] - target
    d_two = prediction[:, 1] - target
    error_cell = 0.375 * (d_one * d_one + d_two * d_two) + 0.25 * d_one * d_two
    loss_part = jnp.sum(cell_weight[None, :, :, None] * error_cell) / normaliser
    cell_scale = cell_weight[None, :, :, None] / normaliser
    g_one = cell_scale * (0.75 * d_one + 0.25 * d_two)
    g_two = cell_scale * (0.75 * d_two + 0.25 * d_one)
    g_pred = jnp.stack([g_one, g_two], axis=1).astype(BF)
    g_branch = spectral(g_pred).astype(BF)
    g_hidden = jnp.einsum("imnlf,hf->imnlh", g_branch, full_out, preferred_element_type=F32)
    sigmoid = jax.nn.sigmoid(pre_act)
    g_pre = (g_hidden * sigmoid * (1.0 + pre_act * (1.0 - sigmoid))).astype(BF)
    grad_in = jnp.einsum("imnlc,imnlh->ch", stacked, g_pre, preferred_element_type=F32)
    grad_out = jnp.einsum("imnlh,imnlf->hf", hidden, g_branch, preferred_element_type=F32)

    k_in, h_in = weight_in.shape
    h_out, f_out = weight_out.shape
    back = exchange(
        [
            grad_in.astype(BF).reshape(lats, k_in, levs, h_in).transpose(0, 2, 1, 3).reshape(devices, -1),
            grad_out.astype(BF).reshape(levs, h_out, lats, f_out).transpose(2, 0, 1, 3).reshape(devices, -1),
            *[every(t[None]) for t in parts_of(loss_part, 3)],
        ],
        devices,
    )
    grad_in = jnp.sum(back[0].astype(F32), axis=0).reshape(k_in, h_in)
    grad_out = jnp.sum(back[1].astype(F32), axis=0).reshape(h_out, f_out)
    loss_value = sum(jnp.sum(b.astype(F32)) for b in back[2:5])
    new_in = adamw(weight_in, moment_in, second_in, grad_in)
    new_out = adamw(weight_out, moment_out, second_out, grad_out)
    return (loss_value, *new_in, *new_out)


def solution(mesh):
    field = P(None, "lat", "lev", None)
    row, first, second = P("lat", None), P("lat", "lev"), P("lev", "lat")
    return jax.shard_map(
        body,
        mesh=mesh,
        in_specs=(field, field, field, row, row, P(), first, second, first, first, second, second),
        out_specs=(P(), first, first, first, second, second, second),
        check_vma=False,
    )
```

time: 1470 us -> 75.9 us (0.05)
  waiting for transfers between devices: 1200 us -> 17.8 us
  blocking collectives: 177 us -> 15.3 us
  matrix products: 40.6 us -> 5.58 us
    reduce_scatter x4 -> x0, waiting for transfers between devices: 865 us -> none  [the longest x2 742 us: spectral(): lax.psum_scatter(jnp.dot(flat_cols, basis_use, preferred_element_type=jnp...]
    all_gather x4 -> x0, waiting for transfers between devices: 339 us -> none  [the longest x2 324 us: spectral(): lax.all_gather(filtered, 'lat', axis=0, tiled=True)]
    all_gather x2 -> x0, blocking collectives: 73.8 us -> none  [the longest x1 43.3 us: body(): lax.all_gather(weight_out.astype(jnp.bfloat16), 'lat', axis=1, tiled=True)]
    psum x2 -> x0, blocking collectives: 62.4 us -> none  [the longest x1 38.6 us: body(): lax.psum(jnp.sum(cell_weight[None, :, None, :] * error_cell) / normaliser...]
    unnamed x1 -> x0, blocking collectives: 40.6 us -> none
    dot_general x8 -> x6, matrix products: 40.6 us -> 5.58 us  [the longest x1 1.99 us: body(): jnp.einsum('imnlc,imnlh->ch', stacked, g_pre, preferred_element_type=F32)]
    all_to_all x0 -> x1, waiting for transfers between devices: none -> 17.8 us  [exchange(): lax.all_to_all(flat.reshape(devices, -1, 128), EVERY, 0, 0, tiled=True)]
    all_to_all x0 -> x1, blocking collectives: none -> 15.3 us  [exchange(): lax.all_to_all(flat.reshape(devices, -1, 128), EVERY, 0, 0, tiled=True)]
  transfers between devices with their start and end apart: 10 -> 1, of which waited for: 7 -> 1; matrix products, arithmetic and copies ran while one was open for 1% -> 0% of each run, Pallas kernels for 0% -> 0%
where the time goes in v1:
time: 75.9 us; the launch traced here: 75.4 us
  waiting for transfers between devices  17.8 us (23%)
  local copies, waits for them, and re-layouts  15.3 us (20%)
  blocking collectives  15.3 us (20%)
  other arithmetic  8.3 us (11%)
  starting transfers between devices  7.51 us (10%)
  between operations  5.65 us (7%)
  matrix products  5.58 us (7%)
    all_to_all x1, waiting for transfers between devices, exchange(): lax.all_to_all(flat.reshape(devices, -1, 128), EVERY, 0, 0, tiled=True)  17.8 us
    all_to_all x1, blocking collectives, exchange(): lax.all_to_all(flat.reshape(devices, -1, 128), EVERY, 0, 0, tiled=True)  15.3 us
    all_to_all x1, starting transfers between devices, exchange(): lax.all_to_all(flat.reshape(devices, -1, 128), EVERY, 0, 0, tiled=True)  7.51 us
    convert_element_type x4, local copies, waits for them, and re-layouts, body(): target = whole(got[1]).astype(F32)  2.5 us
    convert_element_type x3, local copies, waits for them, and re-layouts, body(): state = whole(got[0]).astype(F32)  2.04 us
    dot_general x1, matrix products, body(): jnp.einsum('imnlc,imnlh->ch', stacked, g_pre, preferred_element_type=F32)  1.99 us
    unnamed x26, local copies, waits for them, and re-layouts  1.64 us
  transfers between devices with their start and end apart: 1, of which 1 were waited for; matrix products, arithmetic and copies ran while one was open for 0% of the time, Pallas kernels for 0%

profile of v1, /device:TPU:0, one launch (start us, length us, event | category | flops | bytes accessed | tf_op | source)
XLA Modules:
  0.0 75.4 jit_solution(5260712031756512779)
XLA Ops:
  0.6 1.1 %multiply_reduce_fusion.1 = (f32[2,32]{1,0:T(2,128)S(1)}, bf16[256,2,2,32]{0,3,2,1:T(8,128)(2,1)S(1)}) fusion(f32[2,2,32,256]{3,2,1,0:T(8,128)} %param.14), kind=kLoop, calls=%fused_computation.54 | loop fusion | flops 98240 | bytes 196864 | tf_op jit(solution)/shard_map/reduce_sum | solution.py:83
  1.9 0.7 convert_element_type.231
  2.7 0.9 %fusion.39 = (s32[2]{0:T(128)S(1)}, bf16[256,2]{0,1:T(2,128)(2,1)S(1)}) fusion(s32[2,256]{1,0:T(2,128)} %param.15), kind=kLoop, calls=%fused_computation.86 | loop fusion | flops 1022 | bytes 3080 | tf_op jit(solution)/shard_map/reduce_sum | solution.py:84
  3.6 0.7 convert_element_type.233
  4.5 0.7 convert_element_type.232
  5.8 0.3 reshape_reshape.29
  6.1 0.4 copy.165
  6.5 0.5 reshape_reshape.27
  7.1 0.4 copy.166
  7.5 0.5 reshape_reshape.28
  8.2 0.4 concatenate.9
  8.7 0.9 %copy.208 = bf16[4,8,80,128]{3,2,1,0:T(8,128)(2,1)} copy(bf16[4,8,80,128]{3,1,2,0:T(8,128)(2,1)S(1)} %pad_bitcast_fusion) | data formatting | bytes 1310720
  9.6 7.5 %all-to-all-start = ((bf16[32,80,128]{2,1,0:T(8,128)(2,1)}), bf16[32,80,128]{2,1,0:T(8,128)(2,1)S(1)}, u32[]{:S(2)}, u32[]{:S(2)}) async-start(bf16[32,80,128]{2,1,0:T(8,128)(2,1)} %bitcast.41), calls=%async_computation | async-start | bytes 1310720 | tf_op jit(solution)/shard_map/all_to_all | solution.py:42
  17.1 17.8 %all-to-all-done = bf16[32,80,128]{2,1,0:T(8,128)(2,1)S(1)} async-done(((bf16[32,80,128]{2,1,0:T(8,128)(2,1)}), bf16[32,80,128]{2,1,0:T(8,128)(2,1)S(1)}, u32[]{:S(2)}, u32[]{:S(2)}) %all-to-all-start) | async-done | bytes 655392 | tf_op jit(solution)/shard_map/all_to_all | solution.py:42
  34.9 0.2 copy.227
  35.6 0.9 %reshape.262 = f32[8,4,8,4,2,32]{5,4,3,2,1,0:T(2,128)S(1)} reshape(f32[32,2048]{1,0:T(8,128)S(1)} %get-tuple-element.50) | data formatting | bytes 524288 | tf_op jit(solution)/shard_map/convert_element_type | solution.py:100
  36.5 0.7 copy.183
  37.2 0.5 reshape.258
  37.6 0.5 reshape.257
  38.3 0.7 multiply_reduce_fusion.2
  39.4 0.2 copy.205
  39.6 0.3 reshape_reshape.32
  39.9 0.2 copy.177
  40.1 0.3 reshape.264
  40.4 0.4 reshape_reshape.33
  40.8 0.2 copy.178
  41.1 0.4 reshape.260
  41.6 0.3 copy.171
  41.9 0.3 reshape.255
  42.2 0.9 %reshape.259 = f32[8,4,8,4,2,32]{5,4,3,2,1,0:T(2,128)S(1)} reshape(f32[32,2048]{1,0:T(8,128)S(1)} %get-tuple-element.51) | data formatting | bytes 524288 | tf_op jit(solution)/shard_map/convert_element_type | solution.py:99
  43.1 0.7 copy.170
  43.8 0.5 reshape.254
  44.4 1.4 %multiply_convert_fusion.2 = (bf16[4,2,16,8,256]{4,3,2,1,0:T(8,128)(2,1)S(1)}, f32[4,2,16,8,256]{4,3,2,1,0:T(8,128)}) fusion(bf16[384,256,1,1,1]{1,0,2,3,4:T(8,128)(2,1)S(1)} %reshape.264, bf16[4,2,16,8,128]{4,3,2,1,0:T(8,128)(2,1)S(1)} %get-tuple-element.53, bf16[4,2,16,8,128]{4,3,2,1,0:T(8,128)(2,1)S(1)} %add_convert_fusion, ...), kind=kOutput, calls=%fused_computation.22 | convolution fusion | flops 204996608 | bytes 2555904 | tf_op jit(solution)/shard_map/imnlc,ch->imnlh/dot_general | solution.py:124
  45.9 0.3 convolution_convert_fusion
  46.2 0.8 %fusion.3 = f32[4,2,8,128,16]{3,4,2,1,0:T(8,128)S(1)} fusion(bf16[16,86,1,1,1]{1,0,4,3,2:T(8,128)(2,1)S(1)} %bitcast.146, f32[86]{0:T(128)S(1)} %copy-done.8, bf16[4,2,16,8,128]{4,3,2,1,0:T(8,128)(2,1)S(1)} %convolution_convert_fusion), kind=kOutput, calls=%fused_computation.5 | convolution fusion | flops 46497792 | bytes 789528 | tf_op jit(solution)/shard_map/nk,imklf->imnlf/dot_general | solution.py:122
  46.9 0.2 bitcast_add_fusion
  47.9 0.7 multiply_reduce_fusion
  49.4 0.8 %fusion.12 = bf16[4,2,16,8,128]{4,2,3,1,0:T(8,128)(2,1)S(1)} fusion(bf16[16,86,1,1,1]{1,0,4,3,2:T(8,128)(2,1)S(1)} %bitcast.147, f32[86]{0:T(128)S(1)} %copy-done.8, bf16[4,2,16,8,128]{4,3,2,0,1:T(8,128)(2,1)S(1)} %pad_maximum_fusion.3), kind=kOutput, calls=%fused_computation.16 | convolution fusion | flops 46628864 | bytes 527384 | tf_op jit(solution)/shard_map/nk,imklf->imnlf/dot_general | solution.py:122
  50.2 0.4 fusion.13
  50.6 2.0 %fusion.11 = bf16[384,256]{1,0:T(8,128)(2,1)S(1)} fusion(f32[4,2,16,8,256]{4,3,2,1,0:T(8,128)} %get-tuple-element.59, bf16[4,2,16,8,128]{4,3,2,1,0:T(8,128)(2,1)S(1)} %get-tuple-element.53, bf16[4,2,16,8,128]{4,3,2,1,0:T(8,128)(2,1)S(1)} %add_convert_fusion, bf16[4,2,16,8,128]{4,3,2,1,0:T(8,128)(2,1)S(1)} %get-tuple-element.52, ...), kind=kOutput, calls=%fused_computation.15 | convolution fusion | flops 273252352 | bytes 2359296 | tf_op jit(solution)/shard_map/imnlc,imnlh->ch/dot_general | solution.py:140
  52.8 0.2 reshape.246
  53.1 0.3 reshape.247
  53.3 0.3 copy.191
  53.6 0.8 %reshape.249 = bf16[32,1024]{1,0:T(8,128)(2,1)S(1)} reshape(bf16[8,4,64,16]{3,2,1,0:T(8,128)(2,1)S(1)} %copy.191) | data formatting | bytes 131072 | tf_op jit(solution)/shard_map/reshape | solution.py:148
  54.7 15.3 %all_to_all.10 = bf16[32,40,128]{2,1,0:T(8,128)(2,1)S(1)} all-to-all(bf16[32,40,128]{2,1,0:T(8,128)(2,1)S(1)} %bitcast.135), channel_id=1, replica_groups=mesh['lat'=8,'lev'=4] {'lat','lev'}, dimensions={0} | all-to-all | bytes 655360 | tf_op jit(solution)/shard_map/all_to_all | solution.py:42
  70.0 0.7 convert_reduce_fusion.2
  72.9 0.6 multiply_subtract_fusion.1
  73.6 0.6 multiply_subtract_fusion
  (83 shorter events, 3.6 us)
Async XLA Ops:
  0.6 5.5 %copy-start = (bf16[4,2,32,256]{3,2,1,0:T(8,128)(2,1)S(1)}, bf16[4,2,32,256]{3,2,1,0:T(8,128)(2,1)}, u32[]{:S(2)}) copy-start(bf16[4,2,32,256]{3,2,1,0:T(8,128)(2,1)} %param.12) | copy-start | bytes 393220
  5.3 1.8 %copy-start.1 = (bf16[4,2,32,256]{3,2,1,0:T(8,128)(2,1)S(1)}, bf16[4,2,32,256]{3,2,1,0:T(8,128)(2,1)}, u32[]{:S(2)}) copy-start(bf16[4,2,32,256]{3,2,1,0:T(8,128)(2,1)} %param.13) | copy-start | bytes 393220
  9.6 25.3 %all-to-all-start = ((bf16[32,80,128]{2,1,0:T(8,128)(2,1)}), bf16[32,80,128]{2,1,0:T(8,128)(2,1)S(1)}, u32[]{:S(2)}, u32[]{:S(2)}) async-start(bf16[32,80,128]{2,1,0:T(8,128)(2,1)} %bitcast.41), calls=%async_computation | async-start | bytes 1310720 | tf_op jit(solution)/shard_map/all_to_all | solution.py:42
  44.4 1.7 %copy-start.8 = (f32[86]{0:T(128)S(1)}, f32[86]{0:T(128)}, u32[]{:S(2)}) copy-start(f32[86]{0:T(128)} %param.17) | copy-start | bytes 1036
  54.5 18.4 %copy-start.3 = (f32[64,16]{0,1:T(8,128)S(1)}, f32[64,16]{0,1:T(8,128)}, u32[]{:S(2)}) copy-start(f32[64,16]{0,1:T(8,128)} %param.19) | copy-start | bytes 12292
  54.6 18.4 %copy-start.6 = (f32[64,16]{0,1:T(8,128)S(1)}, f32[64,16]{0,1:T(8,128)}, u32[]{:S(2)}) copy-start(f32[64,16]{0,1:T(8,128)} %param.22) | copy-start | bytes 12292
  54.6 18.4 %copy-start.7 = (f32[64,16]{0,1:T(8,128)S(1)}, f32[64,16]{0,1:T(8,128)}, u32[]{:S(2)}) copy-start(f32[64,16]{0,1:T(8,128)} %param.23) | copy-start | bytes 12292
  54.6 18.9 %copy-start.2 = (f32[48,64]{1,0:T(8,128)S(1)}, f32[48,64]{1,0:T(8,128)}, u32[]{:S(2)}) copy-start(f32[48,64]{1,0:T(8,128)} %param.18) | copy-start | bytes 36868
  54.6 18.9 %copy-start.4 = (f32[48,64]{1,0:T(8,128)S(1)}, f32[48,64]{1,0:T(8,128)}, u32[]{:S(2)}) copy-start(f32[48,64]{1,0:T(8,128)} %param.20) | copy-start | bytes 36868
  54.7 18.9 %copy-start.5 = (f32[48,64]{1,0:T(8,128)S(1)}, f32[48,64]{1,0:T(8,128)}, u32[]{:S(2)}) copy-start(f32[48,64]{1,0:T(8,128)} %param.21) | copy-start | bytes 36868

commit v2 on v1

--- a/solution.py
+++ b/solution.py
@@ -3,6 +3,8 @@
 import jax
 import jax.numpy as jnp
 from jax import lax
+from jax.experimental import pallas as pl
+from jax.experimental.pallas import tpu as pltpu
 from jax.sharding import PartitionSpec as P
 
 STEP = 7
@@ -48,7 +50,7 @@
     return out
 
 
-def body(
+def plain_body(
     column_state,
     column_target,
     member_noise,
@@ -158,9 +160,309 @@
     return (loss_value, *new_in, *new_out)
 
 
+LANES = 128
+SUBLANES = 8
+NT = (((1,), (1,)), ((), ()))
+TN = (((0,), (0,)), ((), ()))
+HIGHEST = lax.Precision.HIGHEST
+
+
+def kernels_fit(arrays, lats, levs):
+    items, rows, feats, lons = arrays[0].shape
+    members, modes = arrays[2].shape[0], arrays[4].shape[1]
+    devices = lats * levs
+    return (
+        lons == devices * SUBLANES
+        and lats * rows * SUBLANES == LANES
+        and (rows, feats, levs, members) == (2, LANES // 4, 4, 2)
+        and items % 2 == 0
+        and lons % LANES == 0
+        and modes < LANES
+        and arrays[6].shape[0] % 16 == 0
+        and arrays[7].shape[1] % 16 == 0
+        and arrays[6].shape[1] == arrays[7].shape[0] == LANES // 2
+    )
+
+
+def lane_index(shape):
+    return lax.broadcasted_iota(jnp.int32, shape, len(shape) - 1)
+
+
+def row_index(shape):
+    return lax.broadcasted_iota(jnp.int32, shape, len(shape) - 2)
+
+
+def halves(top, bottom):
+    first = lane_index(top.shape) < LANES // 2
+    turned_top, turned_bottom = pltpu.roll(top, LANES // 2, 1), pltpu.roll(bottom, LANES // 2, 1)
+    return jnp.where(first, top, turned_bottom), jnp.where(first, turned_top, bottom)
+
+
+def quarters(v):
+    a0, a2 = halves(v[0], v[2])
+    a1, a3 = halves(v[1], v[3])
+    even = lane_index(a0.shape) // 32 % 2 == 0
+
+    def pair(a, b):
+        return jnp.where(even, a, pltpu.roll(b, 32, 1)), jnp.where(even, pltpu.roll(a, 96, 1), b)
+
+    return (*pair(a0, a1), *pair(a2, a3))
+
+
+def pack_kernel(state, target, noise, mask, basis, first, second, send, aux):
+    devices, lons = send.shape[0], state.shape[1]
+    eye = (row_index((lons, lons)) == lane_index((lons, lons))).astype(BF)
+
+    def turned(rows):
+        out = lax.dot_general(eye, rows.astype(BF), NT, preferred_element_type=F32)
+        return [out[:, g : g + LANES].reshape(devices, SUBLANES, LANES) for g in range(0, out.shape[1], LANES)]
+
+    fields = noise[...]
+    groups = turned(state[...]) + turned(target[...]) + turned(fields)
+    start = SUBLANES * len(groups)
+    send[:, :start, :] = jnp.concatenate(groups, axis=1).astype(BF)
+
+    def folded(rows):
+        half = rows.shape[0] // 2
+        return jnp.concatenate([rows[:half], rows[half:]], axis=1)
+
+    weights = jnp.concatenate([folded(first[...]), folded(second[...])], axis=0).astype(BF)
+    send[:, start : start + weights.shape[0], :] = jnp.broadcast_to(weights[None], (devices,) + weights.shape)
+    start += weights.shape[0]
+
+    squares = lax.dot_general(jnp.ones((SUBLANES, lons), F32), fields * fields, NT, precision=HIGHEST)
+    count = squares.shape[1]
+    source, feature = row_index((count, LANES)), lane_index((count, LANES)) % 32
+    sums = []
+    for member in range(2):
+        pick = ((source // 64 == member) & (source % 32 == feature)).astype(F32)
+        total = jnp.dot(squares, pick, precision=HIGHEST)
+        high = total.astype(BF).astype(F32)
+        sums += [high[:1], (total - high)[:1]]
+    cells = mask[...].astype(F32)
+    aux[...] = jnp.zeros_like(aux)
+    aux[0:2, 0 : basis.shape[1]] = basis[...]
+    counts = jnp.sum(cells, axis=1, keepdims=True)
+    top = aux[0:2, :]
+    top = jnp.where(lane_index(top.shape) == LANES - 1, counts, top)
+    share = LANES // SUBLANES
+    for g in range(lons // LANES):
+        block = jnp.concatenate([top, cells[:, g * LANES : (g + 1) * LANES], *sums], axis=0).astype(BF)
+        send[g * share : (g + 1) * share, start:, :] = jnp.broadcast_to(block[None], (share, SUBLANES, LANES))
+
+
+def step_kernel(got, mode_filter, send, weights, stacked, grads, aux, *, items, k_in, k_out, lons):
+    lats, levs = got.shape[0], got.shape[1]
+    block = (LANES, LANES)
+    lat_total = LANES // SUBLANES
+    half_in, half_out = k_in // 2, k_out // 2
+    at_weights = SUBLANES * (items + 1)
+    at_aux = at_weights + half_in + half_out
+    hiddens = 2 * LANES
+    lane, row = lane_index(block), row_index(block)
+
+    for p in range(2):
+        columns = slice(p * LANES, (p + 1) * LANES)
+        for lat in range(lats):
+            one = got[lat, 2 * p, at_weights:at_aux, :].astype(F32)
+            two = got[lat, 2 * p + 1, at_weights:at_aux, :].astype(F32)
+            top, bottom = halves(one, two)
+            a, b = lat * k_in, lats * k_in + lat * k_out
+            weights[a : a + k_in, columns] = jnp.concatenate([top[:half_in], bottom[:half_in]], axis=0).astype(BF)
+            weights[b : b + k_out, columns] = jnp.concatenate([top[half_in:], bottom[half_in:]], axis=0).astype(BF)
+    taps = lats * k_in
+
+    sums = jnp.zeros((4, LANES), F32)
+    for lev in range(levs):
+        total = got[0, lev, at_aux + 4 : at_aux + 8, :].astype(F32)
+        for lat in range(1, lats):
+            total = total + got[lat, lev, at_aux + 4 : at_aux + 8, :].astype(F32)
+        sums = sums + jnp.where(lane_index(total.shape) // 32 == lev, total, 0.0)
+    scale = [
+        lax.rsqrt((sums[2 * m : 2 * m + 1] + sums[2 * m + 1 : 2 * m + 2]) / (lat_total * lons) + 1e-05)
+        for m in range(2)
+    ]
+
+    def spread(first):
+        return jnp.concatenate(
+            [
+                jnp.broadcast_to(got[lat, 0, at_aux + first + n : at_aux + first + n + 1, :].astype(F32), (SUBLANES, LANES))
+                for lat in range(lats)
+                for n in range(2)
+            ],
+            axis=0,
+        )
+
+    basis_rows, mask_rows = spread(0), spread(2)
+    device = lax.axis_index("lat") * levs + lax.axis_index("lev")
+    own = lane == device % lat_total * SUBLANES + row % SUBLANES
+    mask = jnp.dot(jnp.where(own, mask_rows, 0.0).astype(BF), jnp.ones(block, BF), preferred_element_type=F32)
+    latitude = (row // SUBLANES).astype(F32)
+    cosine = jnp.cos((latitude + 0.5) * (math.pi / lat_total) - 0.5 * math.pi)
+    weight_sum = jnp.sum(jnp.where(lane == LANES - 1, cosine * basis_rows, 0.0)) / SUBLANES
+    normaliser = items * LANES * weight_sum
+    cell_weight = cosine * mask
+    cell_scale = cell_weight / normaliser
+
+    modes = mode_filter.shape[1]
+    aux[...] = jnp.zeros_like(aux)
+    aux[0:1, 0:modes] = mode_filter[...]
+    basis = jnp.where(lane < modes, basis_rows, 0.0)
+    operator = lax.dot_general(basis * aux[0:1, :], basis, NT, precision=HIGHEST)
+    operator = jnp.where(row % SUBLANES == lane % SUBLANES, operator, 0.0)
+    high = operator.astype(BF)
+    operator = jnp.concatenate([high, (operator - high.astype(F32)).astype(BF)], axis=1)
+
+    def spectral(v):
+        return jnp.dot(operator, jnp.concatenate([v, v], axis=0), preferred_element_type=F32)
+
+    def field_pair(group):
+        at = slice(group * SUBLANES, (group + 1) * SUBLANES)
+        parts = quarters([got[:, lev, at, :].astype(F32).reshape(lats * SUBLANES, LANES) for lev in range(levs)])
+        parts = [q.reshape(lats, 1, SUBLANES, LANES) for q in parts]
+        return [jnp.concatenate(parts[2 * k : 2 * k + 2], axis=1).reshape(block) for k in range(2)]
+
+    states = [f for g in range(items // 2) for f in field_pair(g)]
+    targets = [f for g in range(items // 2, items) for f in field_pair(g)]
+    scaled = [NOISE_SCALE * (f * scale[m]) for m, f in enumerate(field_pair(items))]
+    edge = jnp.zeros((SUBLANES, LANES), F32)
+
+    def shifted(x, axis_rows=SUBLANES):
+        zeros = jnp.zeros((axis_rows, x.shape[1]), F32)
+        return jnp.concatenate([zeros, x[:-axis_rows]], axis=0), jnp.concatenate([x[axis_rows:], zeros], axis=0)
+
+    for item in range(items):
+        for m in range(2):
+            x = (states[item] + scaled[m]).astype(BF).astype(F32)
+            before, after = shifted(x)
+            at = (2 * item + m) * LANES
+            stacked[at : at + LANES, :] = jnp.concatenate([before, x, after], axis=1).astype(BF)
+
+    first = weights[0:taps, :]
+    second = weights[taps:, :]
+    loss = jnp.zeros(block, F32)
+    for item in range(items):
+        at = slice(2 * item * LANES, 2 * (item + 1) * LANES)
+        x = stacked[at, :]
+        pre_act = jnp.dot(x, first, preferred_element_type=F32)
+        sigmoid = jax.nn.sigmoid(pre_act)
+        hidden = (pre_act * sigmoid).astype(BF)
+        slope = sigmoid * (1.0 + pre_act * (1.0 - sigmoid))
+        branch = lax.dot_general(hidden, second, NT, preferred_element_type=F32).astype(BF)
+        base = states[item]
+        d_one = base + spectral(branch[:LANES]) - targets[item]
+        d_two = base + spectral(branch[LANES:]) - targets[item]
+        loss = loss + (0.375 * (d_one * d_one + d_two * d_two) + 0.25 * d_one * d_two)
+        g_one = (cell_scale * (0.75 * d_one + 0.25 * d_two)).astype(BF)
+        g_two = (cell_scale * (0.75 * d_two + 0.25 * d_one)).astype(BF)
+        g_branch = jnp.concatenate([spectral(g_one), spectral(g_two)], axis=0).astype(BF)
+        g_hidden = jnp.dot(g_branch, second, preferred_element_type=F32)
+        g_pre = (g_hidden * slope).astype(BF)
+        part_in = lax.dot_general(x, g_pre, TN, preferred_element_type=F32)
+        part_out = lax.dot_general(g_branch, hidden, TN, preferred_element_type=F32)
+        if item == 0:
+            grads[0:taps, :] = part_in
+            grads[taps:, :] = part_out
+        else:
+            grads[0:taps, :] += part_in
+            grads[taps:, :] += part_out
+
+    loss_part = jnp.sum(loss * cell_weight, keepdims=True) / normaliser
+    terms = []
+    for _ in range(3):
+        term = loss_part.astype(BF).astype(F32)
+        terms.append(jnp.broadcast_to(term, (1, LANES)))
+        loss_part = loss_part - term
+    terms.append(jnp.zeros((SUBLANES - 3, LANES), F32))
+    terms = jnp.concatenate(terms, axis=0)
+    for p in range(2):
+        columns = slice(p * LANES, (p + 1) * LANES)
+        for lat in range(lats):
+            a, b = lat * k_in, taps + lat * k_out
+            top = jnp.concatenate([grads[a : a + half_in, columns], grads[b : b + half_out, columns]], axis=0)
+            bottom = jnp.concatenate(
+                [grads[a + half_in : a + k_in, columns], grads[b + half_out : b + k_out, columns]], axis=0
+            )
+            for lev, part in zip((2 * p, 2 * p + 1), halves(top, bottom)):
+                send[lat * levs + lev] = jnp.concatenate([part, terms], axis=0).astype(BF)
+
+
+def update_kernel(got, w_in, m_in, v_in, w_out, m_out, v_out, loss, nw_in, nm_in, nv_in, nw_out, nm_out, nv_out):
+    total = jnp.sum(got[...].astype(F32), axis=0)
+    half_in, half_out = w_in.shape[0] // 2, w_out.shape[0] // 2
+    at_loss = half_in + half_out
+
+    def unfolded(rows):
+        return jnp.concatenate([rows[:, : LANES // 2], rows[:, LANES // 2 :]], axis=0)
+
+    new = adamw(w_in[...], m_in[...], v_in[...], unfolded(total[:half_in]))
+    nw_in[...], nm_in[...], nv_in[...] = new
+    new = adamw(w_out[...], m_out[...], v_out[...], unfolded(total[half_in:at_loss]))
+    nw_out[...], nm_out[...], nv_out[...] = new
+    loss[...] = jnp.sum(total[at_loss:, :1], axis=0, keepdims=True)
+
+
+def kernel_body(state, target, noise, mask, basis, mode_filter, w_in, w_out, m_in, v_in, m_out, v_out):
+    items, _, _, lons = state.shape
+    lats, levs = lax.axis_size("lat"), lax.axis_size("lev")
+    devices = lats * levs
+    k_in, k_out = w_in.shape[0], w_out.shape[1]
+    rows = SUBLANES * (items + 1) + (k_in + k_out) // 2 + SUBLANES
+    back_rows = (k_in + k_out) // 2 + SUBLANES
+
+    def shape(dims, kind=F32):
+        return jax.ShapeDtypeStruct(dims, kind)
+
+    send = pl.pallas_call(
+        pack_kernel,
+        out_shape=shape((devices, rows, LANES), BF),
+        scratch_shapes=[pltpu.VMEM((SUBLANES, LANES), F32)],
+        name="pack",
+    )(
+        state.reshape(-1, lons),
+        target.reshape(-1, lons),
+        noise.reshape(-1, lons),
+        mask,
+        basis,
+        w_in,
+        w_out.T,
+    )
+    got = lax.all_to_all(send, EVERY, 0, 0, tiled=True)
+
+    def step(*refs):
+        step_kernel(*refs, items=items, k_in=k_in, k_out=k_out, lons=lons)
+
+    inputs = lats * (k_in + k_out)
+    back = pl.pallas_call(
+        step,
+        out_shape=shape((devices, back_rows, LANES), BF),
+        scratch_shapes=[
+            pltpu.VMEM((inputs, 2 * LANES), BF),
+            pltpu.VMEM((2 * items * LANES, 3 * LANES), BF),
+            pltpu.VMEM((inputs, 2 * LANES), F32),
+            pltpu.VMEM((SUBLANES, LANES), F32),
+        ],
+        name="step",
+    )(got.reshape(lats, levs, rows, LANES), mode_filter[None])
+    back = lax.all_to_all(back, EVERY, 0, 0, tiled=True)
+    wide, tall = shape(w_in.shape), shape(w_out.shape[::-1])
+    loss, *new = pl.pallas_call(
+        update_kernel,
+        out_shape=(shape((1, 1)), wide, wide, wide, tall, tall, tall),
+        name="update",
+    )(back, w_in, m_in, v_in, w_out.T, m_out.T, v_out.T)
+    return (loss.reshape(()), *new[:3], *[n.T for n in new[3:]])
+
+
 def solution(mesh):
     field = P(None, "lat", "lev", None)
     row, first, second = P("lat", None), P("lat", "lev"), P("lev", "lat")
+    lats, levs = mesh.shape["lat"], mesh.shape["lev"]
+
+    def body(*arrays):
+        step = kernel_body if kernels_fit(arrays, lats, levs) else plain_body
+        return step(*arrays)
+
     return jax.shard_map(
         body,
         mesh=mesh,

time: 75.9 us -> 52.3 us (0.69)
  blocking collectives: 15.3 us -> 41 us
  waiting for transfers between devices: 17.8 us -> 0 us
  local copies, waits for them, and re-layouts: 15.3 us -> 0 us
  Pallas kernels: 0 us -> 10.3 us
  other arithmetic: 8.3 us -> 0 us
  starting transfers between devices: 7.51 us -> 0 us
  matrix products: 5.58 us -> 0 us
  between operations: 5.65 us -> 0.64 us
    all_to_all x1 -> x2, blocking collectives: 15.3 us -> 41 us  [the longest x1 25.4 us: kernel_body(): got = lax.all_to_all(send, EVERY, 0, 0, tiled=True)]
    all_to_all x1 -> x0, waiting for transfers between devices: 17.8 us -> none  [exchange(): lax.all_to_all(flat.reshape(devices, -1, 128), EVERY, 0, 0, tiled=True)]
    pallas_call x0 -> x3, Pallas kernels: none -> 10.3 us  [the longest x1 5.91 us: kernel_body(): pl.pallas_call(step, out_shape=shape((devices, back_rows, LANES), BF), sc...]
    all_to_all x1 -> x0, starting transfers between devices: 7.51 us -> none  [exchange(): lax.all_to_all(flat.reshape(devices, -1, 128), EVERY, 0, 0, tiled=True)]
    convert_element_type x14 -> x0, local copies, waits for them, and re-layouts: 5.89 us -> none  [the longest x4 2.5 us: body(): target = whole(got[1]).astype(F32)]
    dot_general x6 -> x0, matrix products: 5.58 us -> none  [the longest x1 1.99 us: body(): jnp.einsum('imnlc,imnlh->ch', stacked, g_pre, preferred_element_type=F32)]
    reduce_sum x8 -> x0, other arithmetic: 4.15 us -> none  [the longest x1 1.1 us: body(): squares = jnp.sum(member_noise * member_noise, axis=(1, 3))]
    another operation x8 -> x0, local copies, waits for them, and re-layouts: 2.29 us -> none  [the longest x4 1.46 us: exchange(): flat = jnp.concatenate([p.reshape(devices, -1) for p in pieces], axis=1)]
  transfers between devices with their start and end apart: 1 -> 0, of which waited for: 1 -> 0; matrix products, arithmetic and copies ran while one was open for 0% -> 0% of each run, Pallas kernels for 0% -> 0%
where the time goes in v2:
time: 52.3 us; the launch traced here: 52 us
  blocking collectives  41 us (78%)
  Pallas kernels  10.3 us (20%)
  between operations  0.64 us (1%)
    all_to_all x1, blocking collectives, kernel_body(): got = lax.all_to_all(send, EVERY, 0, 0, tiled=True)  25.4 us
    all_to_all x1, blocking collectives, kernel_body(): back = lax.all_to_all(back, EVERY, 0, 0, tiled=True)  15.6 us
    pallas_call x1, Pallas kernels, kernel_body(): pl.pallas_call(step, out_shape=shape((devices, back_rows, LANES), BF), sc...  5.91 us
    pallas_call x1, Pallas kernels, kernel_body(): pl.pallas_call(pack_kernel, out_shape=shape((devices, rows, LANES), BF),...  2.61 us
    pallas_call x1, Pallas kernels, kernel_body(): pl.pallas_call(update_kernel, out_shape=(shape((1, 1)), wide, wide, wide,...  1.81 us

profile of v2, /device:TPU:0, one launch (start us, length us, event | category | flops | bytes accessed | tf_op | source)
XLA Modules:
  0.0 52.0 jit_solution(10815676755074037236)
XLA Ops:
  0.6 2.6 %pack.1 = bf16[32,80,128]{2,1,0:T(8,128)(2,1)} custom-call(bf16[256,256]{1,0:T(8,128)(2,1)} %bitcast.13, bf16[256,256]{1,0:T(8,128)(2,1)} %bitcast.14, f32[128,256]{1,0:T(8,128)} %bitcast.15, s32[2,256]{1,0:T(2,128)} %mask.1, f32[2,86]{1,0:T(2,128)} %basis.1, f32[48,64]{1,0:T(8,128)} %w_in.1, f32[16,64]{1,0:T(8,128)} %bitcast.16), custom_call_target="tpu_custom_call" | custom-call | tf_op jit(solution)/shard_map/pack/pallas_call | solution.py:416
  3.2 25.4 %all_to_all.10 = bf16[32,80,128]{2,1,0:T(8,128)(2,1)} all-to-all(bf16[32,80,128]{2,1,0:T(8,128)(2,1)} %pack.1), channel_id=1, replica_groups=mesh['lat'=8,'lev'=4] {'lat','lev'}, dimensions={0} | all-to-all | bytes 1310720 | tf_op jit(solution)/shard_map/all_to_all | solution.py:430
  28.7 5.9 %step.1 = bf16[32,40,128]{2,1,0:T(8,128)(2,1)} custom-call(bf16[8,4,80,128]{3,2,1,0:T(8,128)(2,1)} %bitcast.12, f32[1,86]{1,0:T(1,128)} %bitcast.20), custom_call_target="tpu_custom_call" | custom-call | tf_op jit(solution)/shard_map/step/pallas_call | solution.py:436
  34.6 15.6 %all_to_all.11.got = bf16[32,40,128]{2,1,0:T(8,128)(2,1)} all-to-all(bf16[32,40,128]{2,1,0:T(8,128)(2,1)} %step.1), channel_id=1, replica_groups=mesh['lat'=8,'lev'=4] {'lat','lev'}, dimensions={0} | all-to-all | bytes 655360 | tf_op jit(solution)/shard_map/all_to_all | solution.py:447
  50.2 1.8 %update.1 = (f32[1,1]{1,0:T(1,128)}, f32[48,64]{1,0:T(8,128)}, f32[48,64]{1,0:T(8,128)}, f32[48,64]{1,0:T(8,128)}, f32[16,64]{1,0:T(8,128)}, /*index=5*/f32[16,64]{1,0:T(8,128)}, f32[16,64]{1,0:T(8,128)}) custom-call(bf16[32,40,128]{2,1,0:T(8,128)(2,1)} %all_to_all.11.got, f32[48,64]{1,0:T(8,128)} %w_in.1, f32[48,64]{1,0:T(8,128)} %m_in.1, f32[48,64]{1,0:T(8,128)} %v_in.1, ...), custom_call_target="tpu_custom_call" | custom-call | tf_op jit(solution)/shard_map/update/pallas_call | solution.py:449

commit v3 on v2

--- a/solution.py
+++ b/solution.py
@@ -209,7 +209,12 @@
     return (*pair(a0, a1), *pair(a2, a3))
 
 
-def pack_kernel(state, target, noise, mask, basis, first, second, send, aux):
+def pack_kernel(*refs):
+    sources, send, arrivals, (aux, arrived) = refs[:7], refs[7], refs[8:15], refs[15:]
+    copies = [pltpu.make_async_copy(s, a, arrived.at[n]) for n, (s, a) in enumerate(zip(sources, arrivals))]
+    for copy in copies:
+        copy.start()
+    state, target, noise, mask, basis, first, second = arrivals
     devices, lons = send.shape[0], state.shape[1]
     eye = (row_index((lons, lons)) == lane_index((lons, lons))).astype(BF)
 
@@ -217,6 +222,8 @@
         out = lax.dot_general(eye, rows.astype(BF), NT, preferred_element_type=F32)
         return [out[:, g : g + LANES].reshape(devices, SUBLANES, LANES) for g in range(0, out.shape[1], LANES)]
 
+    for copy in copies:
+        copy.wait()
     fields = noise[...]
     groups = turned(state[...]) + turned(target[...]) + turned(fields)
     start = SUBLANES * len(groups)
@@ -251,14 +258,15 @@
         send[g * share : (g + 1) * share, start:, :] = jnp.broadcast_to(block[None], (share, SUBLANES, LANES))
 
 
-def step_kernel(got, mode_filter, send, weights, stacked, grads, aux, *, items, k_in, k_out, lons):
+def step_kernel(got, mode_filter, send, weights, stacked, hiddens, slopes, grads, aux, arrived, *, items, k_in, k_out, lons, modes):
+    filter_copy = pltpu.make_async_copy(mode_filter, aux.at[0:1, :], arrived)
+    filter_copy.start()
     lats, levs = got.shape[0], got.shape[1]
     block = (LANES, LANES)
     lat_total = LANES // SUBLANES
     half_in, half_out = k_in // 2, k_out // 2
     at_weights = SUBLANES * (items + 1)
     at_aux = at_weights + half_in + half_out
-    hiddens = 2 * LANES
     lane, row = lane_index(block), row_index(block)
 
     for p in range(2):
@@ -283,32 +291,27 @@
         for m in range(2)
     ]
 
-    def spread(first):
-        return jnp.concatenate(
-            [
-                jnp.broadcast_to(got[lat, 0, at_aux + first + n : at_aux + first + n + 1, :].astype(F32), (SUBLANES, LANES))
-                for lat in range(lats)
-                for n in range(2)
-            ],
-            axis=0,
-        )
-
-    basis_rows, mask_rows = spread(0), spread(2)
+    def spread(rows):
+        return jnp.concatenate([jnp.broadcast_to(r, (SUBLANES, LANES)) for r in rows], axis=0)
+
+    tops = [got[lat, 0, at_aux : at_aux + 4, :].astype(F32) for lat in range(lats)]
+    basis_rows = spread([t[n : n + 1] for t in tops for n in range(2)])
+    mask_rows = spread([t[n : n + 1] for t in tops for n in range(2, 4)])
     device = lax.axis_index("lat") * levs + lax.axis_index("lev")
     own = lane == device % lat_total * SUBLANES + row % SUBLANES
     mask = jnp.dot(jnp.where(own, mask_rows, 0.0).astype(BF), jnp.ones(block, BF), preferred_element_type=F32)
-    latitude = (row // SUBLANES).astype(F32)
+    latitude = row_index((lat_total, LANES)).astype(F32)
     cosine = jnp.cos((latitude + 0.5) * (math.pi / lat_total) - 0.5 * math.pi)
+    cosine = spread([cosine[n : n + 1] for n in range(lat_total)])
     weight_sum = jnp.sum(jnp.where(lane == LANES - 1, cosine * basis_rows, 0.0)) / SUBLANES
     normaliser = items * LANES * weight_sum
     cell_weight = cosine * mask
     cell_scale = cell_weight / normaliser
 
-    modes = mode_filter.shape[1]
-    aux[...] = jnp.zeros_like(aux)
-    aux[0:1, 0:modes] = mode_filter[...]
     basis = jnp.where(lane < modes, basis_rows, 0.0)
-    operator = lax.dot_general(basis * aux[0:1, :], basis, NT, precision=HIGHEST)
+    filter_copy.wait()
+    factors = jnp.where(lane_index((1, LANES)) < modes, aux[0:1, :], 0.0)
+    operator = lax.dot_general(basis * factors, basis, NT, precision=HIGHEST)
     operator = jnp.where(row % SUBLANES == lane % SUBLANES, operator, 0.0)
     high = operator.astype(BF)
     operator = jnp.concatenate([high, (operator - high.astype(F32)).astype(BF)], axis=1)
@@ -340,32 +343,44 @@
 
     first = weights[0:taps, :]
     second = weights[taps:, :]
-    loss = jnp.zeros(block, F32)
-    for item in range(items):
-        at = slice(2 * item * LANES, 2 * (item + 1) * LANES)
-        x = stacked[at, :]
-        pre_act = jnp.dot(x, first, preferred_element_type=F32)
+    spans = [slice(2 * item * LANES, 2 * (item + 1) * LANES) for item in range(items)]
+    branches, gradients, errors = {}, {}, []
+
+    def forward(item):
+        pre_act = jnp.dot(stacked[spans[item], :], first, preferred_element_type=F32)
         sigmoid = jax.nn.sigmoid(pre_act)
         hidden = (pre_act * sigmoid).astype(BF)
-        slope = sigmoid * (1.0 + pre_act * (1.0 - sigmoid))
-        branch = lax.dot_general(hidden, second, NT, preferred_element_type=F32).astype(BF)
-        base = states[item]
+        hiddens[spans[item], :] = hidden
+        slopes[spans[item], :] = sigmoid * (1.0 + pre_act * (1.0 - sigmoid))
+        branches[item] = lax.dot_general(hidden, second, NT, preferred_element_type=F32).astype(BF)
+
+    def compare(item):
+        branch, base = branches[item], states[item]
         d_one = base + spectral(branch[:LANES]) - targets[item]
         d_two = base + spectral(branch[LANES:]) - targets[item]
-        loss = loss + (0.375 * (d_one * d_one + d_two * d_two) + 0.25 * d_one * d_two)
+        errors.append(0.375 * (d_one * d_one + d_two * d_two) + 0.25 * d_one * d_two)
         g_one = (cell_scale * (0.75 * d_one + 0.25 * d_two)).astype(BF)
         g_two = (cell_scale * (0.75 * d_two + 0.25 * d_one)).astype(BF)
-        g_branch = jnp.concatenate([spectral(g_one), spectral(g_two)], axis=0).astype(BF)
-        g_hidden = jnp.dot(g_branch, second, preferred_element_type=F32)
-        g_pre = (g_hidden * slope).astype(BF)
-        part_in = lax.dot_general(x, g_pre, TN, preferred_element_type=F32)
-        part_out = lax.dot_general(g_branch, hidden, TN, preferred_element_type=F32)
+        gradients[item] = jnp.concatenate([spectral(g_one), spectral(g_two)], axis=0).astype(BF)
+
+    def backward(item):
+        g_hidden = jnp.dot(gradients[item], second, preferred_element_type=F32)
+        g_pre = (g_hidden * slopes[spans[item], :]).astype(BF)
+        part_in = lax.dot_general(stacked[spans[item], :], g_pre, TN, preferred_element_type=F32)
+        part_out = lax.dot_general(gradients[item], hiddens[spans[item], :], TN, preferred_element_type=F32)
         if item == 0:
             grads[0:taps, :] = part_in
             grads[taps:, :] = part_out
         else:
             grads[0:taps, :] += part_in
             grads[taps:, :] += part_out
+
+    stages = (forward, compare, backward)
+    for turn in range(items + len(stages) - 1):
+        for late, stage in enumerate(stages):
+            if 0 <= turn - late < items:
+                stage(turn - late)
+    loss = sum(errors[1:], errors[0])
 
     loss_part = jnp.sum(loss * cell_weight, keepdims=True) / normaliser
     terms = []
@@ -413,12 +428,7 @@
     def shape(dims, kind=F32):
         return jax.ShapeDtypeStruct(dims, kind)
 
-    send = pl.pallas_call(
-        pack_kernel,
-        out_shape=shape((devices, rows, LANES), BF),
-        scratch_shapes=[pltpu.VMEM((SUBLANES, LANES), F32)],
-        name="pack",
-    )(
+    sources = (
         state.reshape(-1, lons),
         target.reshape(-1, lons),
         noise.reshape(-1, lons),
@@ -427,28 +437,46 @@
         w_in,
         w_out.T,
     )
+    send = pl.pallas_call(
+        pack_kernel,
+        out_shape=shape((devices, rows, LANES), BF),
+        in_specs=[pl.BlockSpec(memory_space=pltpu.HBM)] * len(sources),
+        scratch_shapes=[
+            *[pltpu.VMEM(s.shape, s.dtype) for s in sources],
+            pltpu.VMEM((SUBLANES, LANES), F32),
+            pltpu.SemaphoreType.DMA((len(sources),)),
+        ],
+        name="pack",
+    )(*sources)
     got = lax.all_to_all(send, EVERY, 0, 0, tiled=True)
 
     def step(*refs):
-        step_kernel(*refs, items=items, k_in=k_in, k_out=k_out, lons=lons)
-
-    inputs = lats * (k_in + k_out)
+        step_kernel(*refs, items=items, k_in=k_in, k_out=k_out, lons=lons, modes=modes)
+
+    inputs, cells, modes = lats * (k_in + k_out), 2 * items * LANES, basis.shape[1]
+    padded_filter = jnp.pad(mode_filter[None], ((0, 0), (0, LANES - modes)))
     back = pl.pallas_call(
         step,
         out_shape=shape((devices, back_rows, LANES), BF),
         scratch_shapes=[
             pltpu.VMEM((inputs, 2 * LANES), BF),
-            pltpu.VMEM((2 * items * LANES, 3 * LANES), BF),
+            pltpu.VMEM((cells, 3 * LANES), BF),
+            pltpu.VMEM((cells, 2 * LANES), BF),
+            pltpu.VMEM((cells, 2 * LANES), F32),
             pltpu.VMEM((inputs, 2 * LANES), F32),
             pltpu.VMEM((SUBLANES, LANES), F32),
+            pltpu.SemaphoreType.DMA,
         ],
+        in_specs=[pl.BlockSpec(memory_space=pltpu.VMEM), pl.BlockSpec(memory_space=pltpu.HBM)],
+        compiler_params=pltpu.CompilerParams(vmem_limit_bytes=16 * 2**20),
         name="step",
-    )(got.reshape(lats, levs, rows, LANES), mode_filter[None])
+    )(got.reshape(lats, levs, rows, LANES), padded_filter)
     back = lax.all_to_all(back, EVERY, 0, 0, tiled=True)
     wide, tall = shape(w_in.shape), shape(w_out.shape[::-1])
     loss, *new = pl.pallas_call(
         update_kernel,
         out_shape=(shape((1, 1)), wide, wide, wide, tall, tall, tall),
+        compiler_params=pltpu.CompilerParams(vmem_limit_bytes=8 * 2**20),
         name="update",
     )(back, w_in, m_in, v_in, w_out.T, m_out.T, v_out.T)
     return (loss.reshape(()), *new[:3], *[n.T for n in new[3:]])

time: 52.3 us -> 48.3 us (0.924)
  blocking collectives: 41 us -> 15.3 us
  waiting for transfers between devices: 0 us -> 17.3 us
  starting transfers between devices: 0 us -> 7.33 us
  Pallas kernels: 10.3 us -> 6.69 us
  local copies, waits for them, and re-layouts: 0 us -> 0.69 us
    all_to_all x1 -> x0, blocking collectives: 25.4 us -> none  [kernel_body(): got = lax.all_to_all(send, EVERY, 0, 0, tiled=True)]
    all_to_all x0 -> x1, waiting for transfers between devices: none -> 17.3 us  [kernel_body(): got = lax.all_to_all(send, EVERY, 0, 0, tiled=True)]
    all_to_all x0 -> x1, starting transfers between devices: none -> 7.33 us  [kernel_body(): got = lax.all_to_all(send, EVERY, 0, 0, tiled=True)]
    pallas_call x1, Pallas kernels: 5.91 us -> 3.3 us  [kernel_body(): pl.pallas_call(step, out_shape=shape((devices, back_rows, LANES), BF), sc...]
    pallas_call x1, Pallas kernels: 1.81 us -> 0.77 us  [kernel_body(): pl.pallas_call(update_kernel, out_shape=(shape((1, 1)), wide, wide, wide,...]
    unnamed x0 -> x14, local copies, waits for them, and re-layouts: none -> 0.69 us
  transfers between devices with their start and end apart: 0 -> 1, of which waited for: 0 -> 1; matrix products, arithmetic and copies ran while one was open for 0% -> 0% of each run, Pallas kernels for 0% -> 0%
where the time goes in v3:
time: 48.3 us; the launch traced here: 48 us
  waiting for transfers between devices  17.3 us (36%)
  blocking collectives  15.3 us (32%)
  starting transfers between devices  7.33 us (15%)
  Pallas kernels  6.69 us (14%)
  between operations  0.74 us (2%)
  local copies, waits for them, and re-layouts  0.69 us (1%)
    all_to_all x1, waiting for transfers between devices, kernel_body(): got = lax.all_to_all(send, EVERY, 0, 0, tiled=True)  17.3 us
    all_to_all x1, blocking collectives, kernel_body(): back = lax.all_to_all(back, EVERY, 0, 0, tiled=True)  15.3 us
    all_to_all x1, starting transfers between devices, kernel_body(): got = lax.all_to_all(send, EVERY, 0, 0, tiled=True)  7.33 us
    pallas_call x1, Pallas kernels, kernel_body(): pl.pallas_call(step, out_shape=shape((devices, back_rows, LANES), BF), sc...  3.3 us
    pallas_call x1, Pallas kernels, kernel_body(): pl.pallas_call(pack_kernel, out_shape=shape((devices, rows, LANES), BF),...  2.62 us
  transfers between devices with their start and end apart: 1, of which 1 were waited for; matrix products, arithmetic and copies ran while one was open for 0% of the time, Pallas kernels for 0%

profile of v3, /device:TPU:0, one launch (start us, length us, event | category | flops | bytes accessed | tf_op | source)
XLA Modules:
  0.0 48.0 jit_solution(16595946855693143180)
XLA Ops:
  0.6 2.6 %pack.1 = bf16[32,80,128]{2,1,0:T(8,128)(2,1)} custom-call(bf16[256,256]{1,0:T(8,128)(2,1)} %bitcast.17, bf16[256,256]{1,0:T(8,128)(2,1)} %bitcast.18, f32[128,256]{1,0:T(8,128)} %bitcast.19, s32[2,256]{1,0:T(2,128)} %refs_3_.1, f32[2,86]{1,0:T(2,128)} %refs_4_.1, f32[48,64]{1,0:T(8,128)} %w_in.1, f32[16,64]{1,0:T(8,128)} %bitcast.13), custom_call_target="tpu_custom_call" | custom-call | tf_op jit(solution)/shard_map/pack/pallas_call | solution.py:440
  3.3 7.3 %all-to-all-start = ((bf16[32,80,128]{2,1,0:T(8,128)(2,1)}), bf16[32,80,128]{2,1,0:T(8,128)(2,1)S(1)}, u32[]{:S(2)}, u32[]{:S(2)}) async-start(bf16[32,80,128]{2,1,0:T(8,128)(2,1)} %pack.1), calls=%async_computation | async-start | bytes 1310720 | tf_op jit(solution)/shard_map/all_to_all | solution.py:451
  10.6 0.0 copy-start.6
  10.6 0.6 %copy-done.6 = f32[86]{0:T(128)S(1)} copy-done((f32[86]{0:T(128)S(1)}, f32[86]{0:T(128)}, u32[]{:S(2)}) %copy-start.6) | copy-done | bytes 368
  11.3 17.3 %all-to-all-done = bf16[32,80,128]{2,1,0:T(8,128)(2,1)S(1)} async-done(((bf16[32,80,128]{2,1,0:T(8,128)(2,1)}), bf16[32,80,128]{2,1,0:T(8,128)(2,1)S(1)}, u32[]{:S(2)}, u32[]{:S(2)}) %all-to-all-start) | async-done | bytes 655392 | tf_op jit(solution)/shard_map/all_to_all | solution.py:451
  28.6 3.3 %step.1 = bf16[32,40,128]{2,1,0:T(8,128)(2,1)S(1)} custom-call(bf16[8,4,80,128]{3,2,1,0:T(8,128)(2,1)S(1)} %bitcast.12, f32[1,128]{1,0:T(1,128)S(1)} %pad.4.refs_1_), custom_call_target="tpu_custom_call" | custom-call | tf_op jit(solution)/shard_map/step/pallas_call | solution.py:458
  31.9 0.0 copy-start
  31.9 0.0 copy-start.1
  31.9 0.0 copy-start.2
  31.9 0.0 copy-start.3
  31.9 0.0 copy-start.4
  31.9 0.0 copy-start.5
  32.0 15.3 %all_to_all.10.got = bf16[32,40,128]{2,1,0:T(8,128)(2,1)S(1)} all-to-all(bf16[32,40,128]{2,1,0:T(8,128)(2,1)S(1)} %step.1), channel_id=1, replica_groups=mesh['lat'=8,'lev'=4] {'lat','lev'}, dimensions={0} | all-to-all | bytes 655360 | tf_op jit(solution)/shard_map/all_to_all | solution.py:474
  47.2 0.0 copy-done
  47.2 0.0 copy-done.1
  47.2 0.0 copy-done.2
  47.2 0.0 copy-done.3
  47.2 0.0 copy-done.4
  47.3 0.0 copy-done.5
  47.3 0.8 %update.1 = (f32[1,1]{1,0:T(1,128)}, f32[48,64]{1,0:T(8,128)}, f32[48,64]{1,0:T(8,128)}, f32[48,64]{1,0:T(8,128)}, f32[16,64]{1,0:T(8,128)}, /*index=5*/f32[16,64]{1,0:T(8,128)}, f32[16,64]{1,0:T(8,128)}) custom-call(bf16[32,40,128]{2,1,0:T(8,128)(2,1)S(1)} %all_to_all.10.got, f32[48,64]{1,0:T(8,128)S(1)} %copy-done, f32[48,64]{1,0:T(8,128)S(1)} %copy-done.2, ...), custom_call_target="tpu_custom_call" | custom-call | tf_op jit(solution)/shard_map/update/pallas_call | solution.py:476
  (1 shorter events, 0.0 us)
Async XLA Ops:
  3.3 25.3 %all-to-all-start = ((bf16[32,80,128]{2,1,0:T(8,128)(2,1)}), bf16[32,80,128]{2,1,0:T(8,128)(2,1)S(1)}, u32[]{:S(2)}, u32[]{:S(2)}) async-start(bf16[32,80,128]{2,1,0:T(8,128)(2,1)} %pack.1), calls=%async_computation | async-start | bytes 1310720 | tf_op jit(solution)/shard_map/all_to_all | solution.py:451
  10.6 0.7 %copy-start.6 = (f32[86]{0:T(128)S(1)}, f32[86]{0:T(128)}, u32[]{:S(2)}) copy-start(f32[86]{0:T(128)} %param.17) | copy-start | bytes 1036
  31.9 15.3 %copy-start = (f32[48,64]{1,0:T(8,128)S(1)}, f32[48,64]{1,0:T(8,128)}, u32[]{:S(2)}) copy-start(f32[48,64]{1,0:T(8,128)} %w_in.1) | copy-start | bytes 36868
  31.9 15.3 %copy-start.1 = (f32[64,16]{0,1:T(8,128)S(1)}, f32[64,16]{0,1:T(8,128)}, u32[]{:S(2)}) copy-start(f32[64,16]{0,1:T(8,128)} %param.19) | copy-start | bytes 12292
  31.9 15.3 %copy-start.2 = (f32[48,64]{1,0:T(8,128)S(1)}, f32[48,64]{1,0:T(8,128)}, u32[]{:S(2)}) copy-start(f32[48,64]{1,0:T(8,128)} %m_in.1) | copy-start | bytes 36868
  31.9 15.3 %copy-start.3 = (f32[48,64]{1,0:T(8,128)S(1)}, f32[48,64]{1,0:T(8,128)}, u32[]{:S(2)}) copy-start(f32[48,64]{1,0:T(8,128)} %v_in.1) | copy-start | bytes 36868
  31.9 15.3 %copy-start.4 = (f32[64,16]{0,1:T(8,128)S(1)}, f32[64,16]{0,1:T(8,128)}, u32[]{:S(2)}) copy-start(f32[64,16]{0,1:T(8,128)} %param.22) | copy-start | bytes 12292
  31.9 15.3 %copy-start.5 = (f32[64,16]{0,1:T(8,128)S(1)}, f32[64,16]{0,1:T(8,128)}, u32[]{:S(2)}) copy-start(f32[64,16]{0,1:T(8,128)} %param.23) | copy-start | bytes 12292

commit v4 on v3

--- a/solution.py
+++ b/solution.py
@@ -1,3 +1,4 @@
+import functools
 import math
 
 import jax
@@ -178,7 +179,7 @@
         and items % 2 == 0
         and lons % LANES == 0
         and modes < LANES
-        and arrays[6].shape[0] % 16 == 0
+        and arrays[6].shape[0] == 3 * arrays[7].shape[1]
         and arrays[7].shape[1] % 16 == 0
         and arrays[6].shape[1] == arrays[7].shape[0] == LANES // 2
     )
@@ -210,11 +211,11 @@
 
 
 def pack_kernel(*refs):
-    sources, send, arrivals, (aux, arrived) = refs[:7], refs[7], refs[8:15], refs[15:]
+    sources, send, arrivals, (aux, arrived) = refs[:8], refs[8], refs[9:17], refs[17:]
     copies = [pltpu.make_async_copy(s, a, arrived.at[n]) for n, (s, a) in enumerate(zip(sources, arrivals))]
     for copy in copies:
         copy.start()
-    state, target, noise, mask, basis, first, second = arrivals
+    state, target, noise, mask, basis, mode_filter, first, second = arrivals
     devices, lons = send.shape[0], state.shape[1]
     eye = (row_index((lons, lons)) == lane_index((lons, lons))).astype(BF)
 
@@ -229,95 +230,91 @@
     start = SUBLANES * len(groups)
     send[:, :start, :] = jnp.concatenate(groups, axis=1).astype(BF)
 
-    def folded(rows):
-        half = rows.shape[0] // 2
-        return jnp.concatenate([rows[:half], rows[half:]], axis=1)
-
-    weights = jnp.concatenate([folded(first[...]), folded(second[...])], axis=0).astype(BF)
-    send[:, start : start + weights.shape[0], :] = jnp.broadcast_to(weights[None], (devices,) + weights.shape)
-    start += weights.shape[0]
+    weights = jnp.concatenate([first[...], second[...]], axis=0)
+    quarter = weights.shape[0] // 4
+    folded = [
+        jnp.concatenate([weights[q * quarter : (q + 1) * quarter, h * 32 : (h + 1) * 32] for q in range(4)], axis=1)
+        for h in range(2)
+    ]
+    folded = jnp.stack(folded).astype(BF)
+    pairs = jnp.broadcast_to(folded[None], (devices // 2,) + folded.shape)
+    send[:, start : start + quarter, :] = pairs.reshape(devices, quarter, LANES)
+    start += quarter
 
     squares = lax.dot_general(jnp.ones((SUBLANES, lons), F32), fields * fields, NT, precision=HIGHEST)
     count = squares.shape[1]
-    source, feature = row_index((count, LANES)), lane_index((count, LANES)) % 32
-    sums = []
-    for member in range(2):
-        pick = ((source // 64 == member) & (source % 32 == feature)).astype(F32)
-        total = jnp.dot(squares, pick, precision=HIGHEST)
-        high = total.astype(BF).astype(F32)
-        sums += [high[:1], (total - high)[:1]]
+    source, at = row_index((count, LANES)), lane_index((count, LANES))
+    pick = (source // 64 == at // 64) & (source % 32 == at % 32)
+    total = jnp.dot(squares, pick.astype(F32), precision=HIGHEST)[:1]
+    high = total.astype(BF).astype(F32)
+    sums = jnp.where(lane_index(total.shape) // 32 % 2 == 0, high, total - high)
     cells = mask[...].astype(F32)
+    modes = basis.shape[1]
     aux[...] = jnp.zeros_like(aux)
-    aux[0:2, 0 : basis.shape[1]] = basis[...]
+    aux[0:2, 0:modes] = basis[...].astype(BF).astype(F32) * jnp.sqrt(mode_filter[...])
+    high = aux[0:2, :].astype(BF).astype(F32)
+    low = aux[0:2, :] - high
     counts = jnp.sum(cells, axis=1, keepdims=True)
-    top = aux[0:2, :]
-    top = jnp.where(lane_index(top.shape) == LANES - 1, counts, top)
+    high = jnp.where(lane_index(high.shape) == LANES - 1, counts, high)
+    spare = jnp.zeros((1, LANES), F32)
     share = LANES // SUBLANES
     for g in range(lons // LANES):
-        block = jnp.concatenate([top, cells[:, g * LANES : (g + 1) * LANES], *sums], axis=0).astype(BF)
+        block = jnp.concatenate([high, low, cells[:, g * LANES : (g + 1) * LANES], sums, spare], axis=0).astype(BF)
         send[g * share : (g + 1) * share, start:, :] = jnp.broadcast_to(block[None], (share, SUBLANES, LANES))
 
 
-def step_kernel(got, mode_filter, send, weights, stacked, hiddens, slopes, grads, aux, arrived, *, items, k_in, k_out, lons, modes):
-    filter_copy = pltpu.make_async_copy(mode_filter, aux.at[0:1, :], arrived)
-    filter_copy.start()
+def row_starts(lats, k_in, k_out, quarter):
+    return [
+        [lat * k_in + q * quarter for q in range(k_in // quarter)]
+        + [lats * k_in + lat * k_out + q * quarter for q in range(k_out // quarter)]
+        for lat in range(lats)
+    ]
+
+
+def unfold(half, weights, starts):
+    lats, levs, quarter, _ = half.shape
+    parts = quarters([half[:, lev].astype(F32).reshape(lats * quarter, LANES) for lev in range(levs)])
+    for q, part in enumerate(parts):
+        for lat in range(lats):
+            at = starts[lat][q]
+            weights[at : at + quarter, 0:LANES] = part[lat * quarter : (lat + 1) * quarter].astype(BF)
+
+
+def prepare_kernel(got, stacked, fields, operators, scales, weights, *, items, k_in, k_out, lons, modes):
     lats, levs = got.shape[0], got.shape[1]
+    at_aux = got.shape[2] - SUBLANES
     block = (LANES, LANES)
     lat_total = LANES // SUBLANES
-    half_in, half_out = k_in // 2, k_out // 2
-    at_weights = SUBLANES * (items + 1)
-    at_aux = at_weights + half_in + half_out
     lane, row = lane_index(block), row_index(block)
 
-    for p in range(2):
-        columns = slice(p * LANES, (p + 1) * LANES)
-        for lat in range(lats):
-            one = got[lat, 2 * p, at_weights:at_aux, :].astype(F32)
-            two = got[lat, 2 * p + 1, at_weights:at_aux, :].astype(F32)
-            top, bottom = halves(one, two)
-            a, b = lat * k_in, lats * k_in + lat * k_out
-            weights[a : a + k_in, columns] = jnp.concatenate([top[:half_in], bottom[:half_in]], axis=0).astype(BF)
-            weights[b : b + k_out, columns] = jnp.concatenate([top[half_in:], bottom[half_in:]], axis=0).astype(BF)
-    taps = lats * k_in
-
-    sums = jnp.zeros((4, LANES), F32)
+    quarter = (k_in + k_out) // 4
+    own_half = got[:, :, at_aux - quarter : at_aux, :]
+    unfold(own_half, weights, row_starts(lats, k_in, k_out, quarter))
+
+    sums = []
     for lev in range(levs):
-        total = got[0, lev, at_aux + 4 : at_aux + 8, :].astype(F32)
+        total = got[0, lev, at_aux:, :].astype(F32)
         for lat in range(1, lats):
-            total = total + got[lat, lev, at_aux + 4 : at_aux + 8, :].astype(F32)
-        sums = sums + jnp.where(lane_index(total.shape) // 32 == lev, total, 0.0)
-    scale = [
-        lax.rsqrt((sums[2 * m : 2 * m + 1] + sums[2 * m + 1 : 2 * m + 2]) / (lat_total * lons) + 1e-05)
-        for m in range(2)
-    ]
+            total = total + got[lat, lev, at_aux:, :].astype(F32)
+        sums.append(total)
+    sums = [s[6:7] for s in quarters(sums)]
+    scale = [lax.rsqrt((sums[2 * m] + sums[2 * m + 1]) / (lat_total * lons) + 1e-05) for m in range(2)]
 
     def spread(rows):
         return jnp.concatenate([jnp.broadcast_to(r, (SUBLANES, LANES)) for r in rows], axis=0)
 
-    tops = [got[lat, 0, at_aux : at_aux + 4, :].astype(F32) for lat in range(lats)]
-    basis_rows = spread([t[n : n + 1] for t in tops for n in range(2)])
-    mask_rows = spread([t[n : n + 1] for t in tops for n in range(2, 4)])
+    tops = [got[lat, 0, at_aux:, :].astype(F32) for lat in range(lats)]
+    high = spread([t[n : n + 1] for t in tops for n in range(2)])
+    low = spread([t[n : n + 1] for t in tops for n in range(2, 4)])
+    mask_rows = spread([t[n : n + 1] for t in tops for n in range(4, 6)])
     device = lax.axis_index("lat") * levs + lax.axis_index("lev")
     own = lane == device % lat_total * SUBLANES + row % SUBLANES
     mask = jnp.dot(jnp.where(own, mask_rows, 0.0).astype(BF), jnp.ones(block, BF), preferred_element_type=F32)
     latitude = row_index((lat_total, LANES)).astype(F32)
     cosine = jnp.cos((latitude + 0.5) * (math.pi / lat_total) - 0.5 * math.pi)
     cosine = spread([cosine[n : n + 1] for n in range(lat_total)])
-    weight_sum = jnp.sum(jnp.where(lane == LANES - 1, cosine * basis_rows, 0.0)) / SUBLANES
-    normaliser = items * LANES * weight_sum
-    cell_weight = cosine * mask
-    cell_scale = cell_weight / normaliser
-
-    basis = jnp.where(lane < modes, basis_rows, 0.0)
-    filter_copy.wait()
-    factors = jnp.where(lane_index((1, LANES)) < modes, aux[0:1, :], 0.0)
-    operator = lax.dot_general(basis * factors, basis, NT, precision=HIGHEST)
-    operator = jnp.where(row % SUBLANES == lane % SUBLANES, operator, 0.0)
-    high = operator.astype(BF)
-    operator = jnp.concatenate([high, (operator - high.astype(F32)).astype(BF)], axis=1)
-
-    def spectral(v):
-        return jnp.dot(operator, jnp.concatenate([v, v], axis=0), preferred_element_type=F32)
+    weight_sum = jnp.sum(jnp.where(lane == LANES - 1, cosine * high, 0.0)) / SUBLANES
+    scales[...] = cosine * mask / (items * LANES * weight_sum)
 
     def field_pair(group):
         at = slice(group * SUBLANES, (group + 1) * SUBLANES)
@@ -325,21 +322,40 @@
         parts = [q.reshape(lats, 1, SUBLANES, LANES) for q in parts]
         return [jnp.concatenate(parts[2 * k : 2 * k + 2], axis=1).reshape(block) for k in range(2)]
 
-    states = [f for g in range(items // 2) for f in field_pair(g)]
-    targets = [f for g in range(items // 2, items) for f in field_pair(g)]
     scaled = [NOISE_SCALE * (f * scale[m]) for m, f in enumerate(field_pair(items))]
     edge = jnp.zeros((SUBLANES, LANES), F32)
-
-    def shifted(x, axis_rows=SUBLANES):
-        zeros = jnp.zeros((axis_rows, x.shape[1]), F32)
-        return jnp.concatenate([zeros, x[:-axis_rows]], axis=0), jnp.concatenate([x[axis_rows:], zeros], axis=0)
-
-    for item in range(items):
-        for m in range(2):
-            x = (states[item] + scaled[m]).astype(BF).astype(F32)
-            before, after = shifted(x)
-            at = (2 * item + m) * LANES
-            stacked[at : at + LANES, :] = jnp.concatenate([before, x, after], axis=1).astype(BF)
+    for group in range(items):
+        for k, field in enumerate(field_pair(group)):
+            fields[2 * group + k] = field.astype(BF)
+            if group >= items // 2:
+                continue
+            for m in range(2):
+                x = (field + scaled[m]).astype(BF).astype(F32)
+                before = jnp.concatenate([edge, x[:-SUBLANES]], axis=0)
+                after = jnp.concatenate([x[SUBLANES:], edge], axis=0)
+                at = (2 * (2 * group + k) + m) * LANES
+                stacked[at : at + LANES, :] = jnp.concatenate([before, x, after], axis=1).astype(BF)
+
+    root = jnp.where(lane < modes, high + low, 0.0)
+    operator = lax.dot_general(root, root, NT, precision=HIGHEST)
+    operator = jnp.where(row % SUBLANES == lane % SUBLANES, operator, 0.0)
+    high = operator.astype(BF)
+    operators[...] = jnp.concatenate([high, (operator - high.astype(F32)).astype(BF)], axis=1)
+
+
+def step_kernel(
+    other, stacked, fields, operators, scales, own, give, keep, losses, weights, hiddens, slopes, g_pres, grads, *, items, k_in, k_out
+):
+    lats, levs, quarter, _ = other.shape
+    taps = lats * k_in
+    starts = row_starts(lats, k_in, k_out, quarter)
+    unfold(other[...], weights, starts)
+    weights[:, LANES:] = own[...]
+
+    operator, cell_scale = operators[...], scales[...]
+
+    def spectral(v):
+        return jnp.dot(operator, jnp.concatenate([v, v], axis=0), preferred_element_type=F32)
 
     first = weights[0:taps, :]
     second = weights[taps:, :]
@@ -355,9 +371,9 @@
         branches[item] = lax.dot_general(hidden, second, NT, preferred_element_type=F32).astype(BF)
 
     def compare(item):
-        branch, base = branches[item], states[item]
-        d_one = base + spectral(branch[:LANES]) - targets[item]
-        d_two = base + spectral(branch[LANES:]) - targets[item]
+        branch, base, target = branches[item], fields[item].astype(F32), fields[items + item].astype(F32)
+        d_one = base + spectral(branch[:LANES]) - target
+        d_two = base + spectral(branch[LANES:]) - target
         errors.append(0.375 * (d_one * d_one + d_two * d_two) + 0.25 * d_one * d_two)
         g_one = (cell_scale * (0.75 * d_one + 0.25 * d_two)).astype(BF)
         g_two = (cell_scale * (0.75 * d_two + 0.25 * d_one)).astype(BF)
@@ -365,15 +381,7 @@
 
     def backward(item):
         g_hidden = jnp.dot(gradients[item], second, preferred_element_type=F32)
-        g_pre = (g_hidden * slopes[spans[item], :]).astype(BF)
-        part_in = lax.dot_general(stacked[spans[item], :], g_pre, TN, preferred_element_type=F32)
-        part_out = lax.dot_general(gradients[item], hiddens[spans[item], :], TN, preferred_element_type=F32)
-        if item == 0:
-            grads[0:taps, :] = part_in
-            grads[taps:, :] = part_out
-        else:
-            grads[0:taps, :] += part_in
-            grads[taps:, :] += part_out
+        g_pres[spans[item], :] = (g_hidden * slopes[spans[item], :]).astype(BF)
 
     stages = (forward, compare, backward)
     for turn in range(items + len(stages) - 1):
@@ -381,51 +389,62 @@
             if 0 <= turn - late < items:
                 stage(turn - late)
     loss = sum(errors[1:], errors[0])
-
-    loss_part = jnp.sum(loss * cell_weight, keepdims=True) / normaliser
+    grads[0:taps, :] = lax.dot_general(stacked[...], g_pres[...], TN, preferred_element_type=F32)
+    g_branch = jnp.concatenate([gradients[item] for item in range(items)], axis=0)
+    grads[taps:, :] = lax.dot_general(g_branch, hiddens[...], TN, preferred_element_type=F32)
+
+    loss_part = jnp.sum(loss * cell_scale, keepdims=True)
     terms = []
     for _ in range(3):
         term = loss_part.astype(BF).astype(F32)
         terms.append(jnp.broadcast_to(term, (1, LANES)))
         loss_part = loss_part - term
     terms.append(jnp.zeros((SUBLANES - 3, LANES), F32))
-    terms = jnp.concatenate(terms, axis=0)
-    for p in range(2):
+    losses[...] = jnp.concatenate(terms, axis=0).astype(BF)
+    for p, half in enumerate((give, keep)):
         columns = slice(p * LANES, (p + 1) * LANES)
-        for lat in range(lats):
-            a, b = lat * k_in, taps + lat * k_out
-            top = jnp.concatenate([grads[a : a + half_in, columns], grads[b : b + half_out, columns]], axis=0)
-            bottom = jnp.concatenate(
-                [grads[a + half_in : a + k_in, columns], grads[b + half_out : b + k_out, columns]], axis=0
-            )
-            for lev, part in zip((2 * p, 2 * p + 1), halves(top, bottom)):
-                send[lat * levs + lev] = jnp.concatenate([part, terms], axis=0).astype(BF)
+        parts = [
+            jnp.concatenate([grads[s[q] : s[q] + quarter, columns] for s in starts], axis=0) for q in range(4)
+        ]
+        for lev, part in enumerate(quarters(parts)):
+            half[:, lev] = part.reshape(lats, quarter, LANES).astype(half.dtype)
+
+
+def join_kernel(keep, came, losses, send):
+    quarter = keep.shape[2]
+    total = (keep[...] + came[...].astype(F32)).astype(BF)
+    send[:, :quarter, :] = total.reshape(-1, quarter, LANES)
+    send[:, quarter:, :] = jnp.broadcast_to(losses[...][None], (send.shape[0], SUBLANES, LANES))
 
 
 def update_kernel(got, w_in, m_in, v_in, w_out, m_out, v_out, loss, nw_in, nm_in, nv_in, nw_out, nm_out, nv_out):
     total = jnp.sum(got[...].astype(F32), axis=0)
-    half_in, half_out = w_in.shape[0] // 2, w_out.shape[0] // 2
-    at_loss = half_in + half_out
+    at_loss = total.shape[1] - SUBLANES
 
     def unfolded(rows):
-        return jnp.concatenate([rows[:, : LANES // 2], rows[:, LANES // 2 :]], axis=0)
-
-    new = adamw(w_in[...], m_in[...], v_in[...], unfolded(total[:half_in]))
-    nw_in[...], nm_in[...], nv_in[...] = new
-    new = adamw(w_out[...], m_out[...], v_out[...], unfolded(total[half_in:at_loss]))
-    nw_out[...], nm_out[...], nv_out[...] = new
-    loss[...] = jnp.sum(total[at_loss:, :1], axis=0, keepdims=True)
+        return jnp.concatenate([rows[:, q * 32 : (q + 1) * 32] for q in range(4)], axis=0)
+
+    gradient = jnp.concatenate([unfolded(total[h, :at_loss]) for h in range(2)], axis=1)
+    k_in = w_in.shape[0]
+    nw_in[...], nm_in[...], nv_in[...] = adamw(w_in[...], m_in[...], v_in[...], gradient[:k_in])
+    nw_out[...], nm_out[...], nv_out[...] = adamw(w_out[...], m_out[...], v_out[...], gradient[k_in:])
+    loss[...] = jnp.sum(total[0, at_loss:, :1] + total[1, at_loss:, :1], axis=0, keepdims=True)
 
 
 def kernel_body(state, target, noise, mask, basis, mode_filter, w_in, w_out, m_in, v_in, m_out, v_out):
     items, _, _, lons = state.shape
     lats, levs = lax.axis_size("lat"), lax.axis_size("lev")
     devices = lats * levs
-    k_in, k_out = w_in.shape[0], w_out.shape[1]
-    rows = SUBLANES * (items + 1) + (k_in + k_out) // 2 + SUBLANES
-    back_rows = (k_in + k_out) // 2 + SUBLANES
-
-    def shape(dims, kind=F32):
+    k_in, k_out, modes = w_in.shape[0], w_out.shape[1], basis.shape[1]
+    quarter = (k_in + k_out) // 4
+    at_weights = SUBLANES * (items + 1)
+    rows = at_weights + quarter + SUBLANES
+    inputs, cells = lats * (k_in + k_out), 2 * items * LANES
+    partners = [(i, i ^ 1) for i in range(levs)]
+    vmem, hbm = pl.BlockSpec(memory_space=pltpu.VMEM), pl.BlockSpec(memory_space=pltpu.HBM)
+    small = pltpu.CompilerParams(vmem_limit_bytes=8 * 2**20)
+
+    def shape(*dims, kind=F32):
         return jax.ShapeDtypeStruct(dims, kind)
 
     sources = (
@@ -434,13 +453,14 @@
         noise.reshape(-1, lons),
         mask,
         basis,
+        mode_filter[None],
         w_in,
         w_out.T,
     )
     send = pl.pallas_call(
         pack_kernel,
-        out_shape=shape((devices, rows, LANES), BF),
-        in_specs=[pl.BlockSpec(memory_space=pltpu.HBM)] * len(sources),
+        out_shape=shape(devices, rows, LANES, kind=BF),
+        in_specs=[hbm] * len(sources),
         scratch_shapes=[
             *[pltpu.VMEM(s.shape, s.dtype) for s in sources],
             pltpu.VMEM((SUBLANES, LANES), F32),
@@ -448,37 +468,52 @@
         ],
         name="pack",
     )(*sources)
-    got = lax.all_to_all(send, EVERY, 0, 0, tiled=True)
-
-    def step(*refs):
-        step_kernel(*refs, items=items, k_in=k_in, k_out=k_out, lons=lons, modes=modes)
-
-    inputs, cells, modes = lats * (k_in + k_out), 2 * items * LANES, basis.shape[1]
-    padded_filter = jnp.pad(mode_filter[None], ((0, 0), (0, LANES - modes)))
-    back = pl.pallas_call(
-        step,
-        out_shape=shape((devices, back_rows, LANES), BF),
+    got = lax.all_to_all(send, EVERY, 0, 0, tiled=True).reshape(lats, levs, rows, LANES)
+    own = got[:, :, at_weights : at_weights + quarter]
+    other = lax.ppermute(own, "lev", partners)
+    prepared = pl.pallas_call(
+        functools.partial(prepare_kernel, items=items, k_in=k_in, k_out=k_out, lons=lons, modes=modes),
+        out_shape=(
+            shape(cells, 3 * LANES, kind=BF),
+            shape(2 * items, LANES, LANES, kind=BF),
+            shape(LANES, 2 * LANES, kind=BF),
+            shape(LANES, LANES),
+            shape(inputs, LANES, kind=BF),
+        ),
+        in_specs=[vmem],
+        compiler_params=small,
+        cost_estimate=pl.CostEstimate(flops=2**22, bytes_accessed=2**22, transcendentals=0),
+        name="prepare",
+    )(got)
+    block = (lats, levs, quarter, LANES)
+    give, keep, losses = pl.pallas_call(
+        functools.partial(step_kernel, items=items, k_in=k_in, k_out=k_out),
+        out_shape=(shape(*block, kind=BF), shape(*block), shape(SUBLANES, LANES, kind=BF)),
         scratch_shapes=[
             pltpu.VMEM((inputs, 2 * LANES), BF),
-            pltpu.VMEM((cells, 3 * LANES), BF),
             pltpu.VMEM((cells, 2 * LANES), BF),
             pltpu.VMEM((cells, 2 * LANES), F32),
+            pltpu.VMEM((cells, 2 * LANES), BF),
             pltpu.VMEM((inputs, 2 * LANES), F32),
-            pltpu.VMEM((SUBLANES, LANES), F32),
-            pltpu.SemaphoreType.DMA,
         ],
-        in_specs=[pl.BlockSpec(memory_space=pltpu.VMEM), pl.BlockSpec(memory_space=pltpu.HBM)],
         compiler_params=pltpu.CompilerParams(vmem_limit_bytes=16 * 2**20),
         name="step",
-    )(got.reshape(lats, levs, rows, LANES), padded_filter)
+    )(other, *prepared)
+    came = lax.ppermute(give, "lev", partners)
+    back = pl.pallas_call(
+        join_kernel,
+        out_shape=shape(devices, quarter + SUBLANES, LANES, kind=BF),
+        compiler_params=small,
+        name="join",
+    )(keep, came, losses)
     back = lax.all_to_all(back, EVERY, 0, 0, tiled=True)
-    wide, tall = shape(w_in.shape), shape(w_out.shape[::-1])
+    wide, tall = shape(*w_in.shape), shape(*w_out.shape[::-1])
     loss, *new = pl.pallas_call(
         update_kernel,
-        out_shape=(shape((1, 1)), wide, wide, wide, tall, tall, tall),
-        compiler_params=pltpu.CompilerParams(vmem_limit_bytes=8 * 2**20),
+        out_shape=(shape(1, 1), wide, wide, wide, tall, tall, tall),
+        compiler_params=small,
         name="update",
-    )(back, w_in, m_in, v_in, w_out.T, m_out.T, v_out.T)
+    )(back.reshape(-1, 2, quarter + SUBLANES, LANES), w_in, m_in, v_in, w_out.T, m_out.T, v_out.T)
     return (loss.reshape(()), *new[:3], *[n.T for n in new[3:]])
 
 

time: 48.3 us -> 44.9 us (0.930)
  blocking collectives: 15.3 us -> 34.7 us
  waiting for transfers between devices: 17.3 us -> 1.73 us
  starting transfers between devices: 7.33 us -> 0.28 us
  local copies, waits for them, and re-layouts: 0.69 us -> 0.06 us
    all_to_all x0 -> x1, blocking collectives: none -> 23 us  [kernel_body(): lax.all_to_all(send, EVERY, 0, 0, tiled=True)]
    all_to_all x1 -> x0, waiting for transfers between devices: 17.3 us -> none  [kernel_body(): got = lax.all_to_all(send, EVERY, 0, 0, tiled=True)]
    all_to_all x1 -> x0, starting transfers between devices: 7.33 us -> none  [kernel_body(): got = lax.all_to_all(send, EVERY, 0, 0, tiled=True)]
    all_to_all x1, blocking collectives: 15.3 us -> 11.7 us  [kernel_body(): back = lax.all_to_all(back, EVERY, 0, 0, tiled=True)]
    ppermute x0 -> x2, waiting for transfers between devices: none -> 1.73 us  [the longest x1 1.2 us: kernel_body(): came = lax.ppermute(give, 'lev', partners)]
    unnamed x14 -> x12, local copies, waits for them, and re-layouts: 0.69 us -> 0.04 us
    pallas_call x3 -> x5, Pallas kernels: 6.69 us -> 7.11 us  [the longest x1 2.93 us: kernel_body(): pl.pallas_call(functools.partial(step_kernel, items=items, k_in=k_in, k_o...]
  transfers between devices with their start and end apart: 1 -> 2, of which waited for: 1 -> 2; matrix products, arithmetic and copies ran while one was open for 0% -> 0% of each run, Pallas kernels for 0% -> 2%
where the time goes in v4:
time: 44.9 us; the launch traced here: 44.6 us
  blocking collectives  34.7 us (77%)
  Pallas kernels  7.11 us (16%)
  waiting for transfers between devices  1.73 us (4%)
  between operations  0.75 us (2%)
    all_to_all x1, blocking collectives, kernel_body(): lax.all_to_all(send, EVERY, 0, 0, tiled=True)  23 us
    all_to_all x1, blocking collectives, kernel_body(): back = lax.all_to_all(back, EVERY, 0, 0, tiled=True)  11.7 us
    pallas_call x1, Pallas kernels, kernel_body(): pl.pallas_call(functools.partial(step_kernel, items=items, k_in=k_in, k_o...  2.93 us
    pallas_call x1, Pallas kernels, kernel_body(): pl.pallas_call(pack_kernel, out_shape=shape(devices, rows, LANES, kind=BF...  2.55 us
    ppermute x1, waiting for transfers between devices, kernel_body(): came = lax.ppermute(give, 'lev', partners)  1.2 us
  transfers between devices with their start and end apart: 2, of which 2 were waited for; matrix products, arithmetic and copies ran while one was open for 0% of the time, Pallas kernels for 2%

profile of v4, /device:TPU:0, one launch (start us, length us, event | category | flops | bytes accessed | tf_op | source)
XLA Modules:
  0.0 44.6 jit_solution(13601424266161679911)
XLA Ops:
  0.6 2.5 %pack.1 = bf16[32,64,128]{2,1,0:T(8,128)(2,1)} custom-call(bf16[256,256]{1,0:T(8,128)(2,1)} %bitcast.20, bf16[256,256]{1,0:T(8,128)(2,1)} %bitcast.21, f32[128,256]{1,0:T(8,128)} %bitcast.22, s32[2,256]{1,0:T(2,128)} %refs_3_.1, f32[2,86]{1,0:T(2,128)} %refs_4_.1, f32[1,86]{1,0:T(1,128)} %bitcast.23, f32[48,64]{1,0:T(8,128)} %w_in.1, f32[16,64]{1,0:T(8,128)} %bitcast.16), custom_call_target="tpu_custom_call" | custom-call | tf_op jit(solution)/shard_map/pack/pallas_call | solution.py:460
  3.2 23.0 %all_to_all.10 = bf16[32,64,128]{2,1,0:T(8,128)(2,1)S(1)} all-to-all(bf16[32,64,128]{2,1,0:T(8,128)(2,1)} %pack.1), channel_id=1, replica_groups=mesh['lat'=8,'lev'=4] {'lat','lev'}, dimensions={0} | all-to-all | bytes 1048576 | tf_op jit(solution)/shard_map/all_to_all | solution.py:471
  26.2 0.1 collective-permute-start
  26.2 0.8 %prepare.1 = (bf16[1024,384]{1,0:T(8,128)(2,1)S(1)}, bf16[8,128,128]{2,1,0:T(8,128)(2,1)S(1)}, bf16[128,256]{1,0:T(8,128)(2,1)S(1)}, f32[128,128]{1,0:T(8,128)S(1)}, bf16[512,128]{1,0:T(8,128)(2,1)S(1)}) custom-call(bf16[8,4,64,128]{3,2,1,0:T(8,128)(2,1)S(1)} %bitcast.14), custom_call_target="tpu_custom_call" | custom-call | flops 4194304 | bytes 4194304 | tf_op jit(solution)/shard_map/prepare/pallas_call | solution.py:474
  27.1 0.5 %collective-permute-done.other = bf16[8,4,16,128]{3,2,1,0:T(8,128)(2,1)S(1)} collective-permute-done((bf16[8,4,16,128]{3,2,1,0:T(8,128)(2,1)S(1)}, bf16[8,4,16,128]{3,2,1,0:T(8,128)(2,1)S(1)}, u32[]{:S(2)}, u32[]{:S(2)}) %collective-permute-start) | collective-permute-done | bytes 131104 | tf_op jit(solution)/shard_map/ppermute | solution.py:473
  27.6 2.9 %step.1 = (bf16[8,4,16,128]{3,2,1,0:T(8,128)(2,1)S(1)}, f32[8,4,16,128]{3,2,1,0:T(8,128)S(1)}, bf16[8,128]{1,0:T(8,128)(2,1)S(1)}) custom-call(bf16[8,4,16,128]{3,2,1,0:T(8,128)(2,1)S(1)} %collective-permute-done.other, bf16[1024,384]{1,0:T(8,128)(2,1)S(1)} %get-tuple-element.22.stacked, bf16[8,128,128]{2,1,0:T(8,128)(2,1)S(1)} %get-tuple-element.23.fields, ...), custom_call_target="tpu_custom_call" | custom-call | tf_op jit(solution)/shard_map/step/pallas_call | solution.py:489
  30.5 0.2 collective-permute-start.1
  30.7 1.2 %collective-permute-done.1.came = bf16[8,4,16,128]{3,2,1,0:T(8,128)(2,1)S(1)} collective-permute-done((bf16[8,4,16,128]{3,2,1,0:T(8,128)(2,1)S(1)}, bf16[8,4,16,128]{3,2,1,0:T(8,128)(2,1)S(1)}, u32[]{:S(2)}, u32[]{:S(2)}) %collective-permute-start.1) | collective-permute-done | bytes 131104 | tf_op jit(solution)/shard_map/ppermute | solution.py:502
  32.0 0.0 copy-start
  32.0 0.0 copy-start.1
  32.0 0.0 copy-start.2
  32.0 0.0 copy-start.3
  32.0 0.0 copy-start.4
  32.0 0.0 copy-start.5
  32.0 11.7 %all_to_all.11 = bf16[32,24,128]{2,1,0:T(8,128)(2,1)S(1)} all-to-all(bf16[32,24,128]{2,1,0:T(8,128)(2,1)S(1)} %join.1), channel_id=1, replica_groups=mesh['lat'=8,'lev'=4] {'lat','lev'}, dimensions={0} | all-to-all | bytes 393216 | tf_op jit(solution)/shard_map/all_to_all | solution.py:509
  43.8 0.0 copy-done
  43.8 0.0 copy-done.1
  43.8 0.0 copy-done.2
  43.8 0.0 copy-done.3
  43.8 0.0 copy-done.4
  43.8 0.0 copy-done.5
  43.8 0.8 %update.1 = (f32[1,1]{1,0:T(1,128)}, f32[48,64]{1,0:T(8,128)}, f32[48,64]{1,0:T(8,128)}, f32[48,64]{1,0:T(8,128)}, f32[16,64]{1,0:T(8,128)}, /*index=5*/f32[16,64]{1,0:T(8,128)}, f32[16,64]{1,0:T(8,128)}) custom-call(bf16[16,2,24,128]{3,2,1,0:T(8,128)(2,1)S(1)} %bitcast.15, f32[48,64]{1,0:T(8,128)S(1)} %copy-done, f32[48,64]{1,0:T(8,128)S(1)} %copy-done.2, ...), custom_call_target="tpu_custom_call" | custom-call | tf_op jit(solution)/shard_map/update/pallas_call | solution.py:511
  (2 shorter events, 0.0 us)
Async XLA Ops:
  26.2 1.4 %collective-permute-start = (bf16[8,4,16,128]{3,2,1,0:T(8,128)(2,1)S(1)}, bf16[8,4,16,128]{3,2,1,0:T(8,128)(2,1)S(1)}, u32[]{:S(2)}, u32[]{:S(2)}) collective-permute-start(bf16[8,4,16,128]{3,2,1,0:T(8,128)(2,1)S(1)} %slice.4), channel_id=1, source_target_pairs={{0,1},{1,0},{2,3},{3,2},{4,5},{5,4},{6,7},{7,6},{8,9},{9,8},{10,11... | collective-permute-start | bytes 393224 | tf_op jit(solution)/shard_map/ppermute | solution.py:473
  30.5 1.4 %collective-permute-start.1 = (bf16[8,4,16,128]{3,2,1,0:T(8,128)(2,1)S(1)}, bf16[8,4,16,128]{3,2,1,0:T(8,128)(2,1)S(1)}, u32[]{:S(2)}, u32[]{:S(2)}) collective-permute-start(bf16[8,4,16,128]{3,2,1,0:T(8,128)(2,1)S(1)} %get-tuple-element.28), channel_id=1, source_target_pairs={{0,1},{1,0},{2,3},{3,2},{4,5},{5,4},{6,7},{7,6},{8,9},{9,8},{10,11... | collective-permute-start | bytes 393224 | tf_op jit(solution)/shard_map/ppermute | solution.py:502
  32.0 11.8 %copy-start = (f32[48,64]{1,0:T(8,128)S(1)}, f32[48,64]{1,0:T(8,128)}, u32[]{:S(2)}) copy-start(f32[48,64]{1,0:T(8,128)} %w_in.1) | copy-start | bytes 36868
  32.0 11.8 %copy-start.1 = (f32[64,16]{0,1:T(8,128)S(1)}, f32[64,16]{0,1:T(8,128)}, u32[]{:S(2)}) copy-start(f32[64,16]{0,1:T(8,128)} %param.19) | copy-start | bytes 12292
  32.0 11.8 %copy-start.2 = (f32[48,64]{1,0:T(8,128)S(1)}, f32[48,64]{1,0:T(8,128)}, u32[]{:S(2)}) copy-start(f32[48,64]{1,0:T(8,128)} %m_in.1) | copy-start | bytes 36868
  32.0 11.8 %copy-start.3 = (f32[48,64]{1,0:T(8,128)S(1)}, f32[48,64]{1,0:T(8,128)}, u32[]{:S(2)}) copy-start(f32[48,64]{1,0:T(8,128)} %v_in.1) | copy-start | bytes 36868
  32.0 11.8 %copy-start.4 = (f32[64,16]{0,1:T(8,128)S(1)}, f32[64,16]{0,1:T(8,128)}, u32[]{:S(2)}) copy-start(f32[64,16]{0,1:T(8,128)} %param.22) | copy-start | bytes 12292
  32.0 11.8 %copy-start.5 = (f32[64,16]{0,1:T(8,128)S(1)}, f32[64,16]{0,1:T(8,128)}, u32[]{:S(2)}) copy-start(f32[64,16]{0,1:T(8,128)} %param.23) | copy-start | bytes 12292

commit v5 on v4

--- a/solution.py
+++ b/solution.py
@@ -241,13 +241,14 @@
     send[:, start : start + quarter, :] = pairs.reshape(devices, quarter, LANES)
     start += quarter
 
-    squares = lax.dot_general(jnp.ones((SUBLANES, lons), F32), fields * fields, NT, precision=HIGHEST)
-    count = squares.shape[1]
-    source, at = row_index((count, LANES)), lane_index((count, LANES))
-    pick = (source // 64 == at // 64) & (source % 32 == at % 32)
-    total = jnp.dot(squares, pick.astype(F32), precision=HIGHEST)[:1]
-    high = total.astype(BF).astype(F32)
-    sums = jnp.where(lane_index(total.shape) // 32 % 2 == 0, high, total - high)
+    squares = noise[...] * noise[...]
+    upper = squares.astype(BF)
+    terms = jnp.concatenate([upper, (squares - upper.astype(F32)).astype(BF)], axis=1)
+    total = lax.dot_general(jnp.ones((SUBLANES, 2 * lons), BF), terms, NT, preferred_element_type=F32)
+    even = lane_index(total.shape) // 32 % 2 == 0
+    total = total + jnp.where(even, pltpu.roll(total, 96, 1), pltpu.roll(total, 32, 1))
+    upper = total.astype(BF).astype(F32)
+    sums = jnp.where(even, upper, total - upper)[:1]
     cells = mask[...].astype(F32)
     modes = basis.shape[1]
     aux[...] = jnp.zeros_like(aux)
@@ -354,40 +355,52 @@
 
     operator, cell_scale = operators[...], scales[...]
 
-    def spectral(v):
-        return jnp.dot(operator, jnp.concatenate([v, v], axis=0), preferred_element_type=F32)
+    def spectral(one, two):
+        v = jnp.concatenate([one, two], axis=1)
+        out = jnp.dot(operator, jnp.concatenate([v, v], axis=0), preferred_element_type=F32)
+        return out[:, :LANES], out[:, LANES:]
 
     first = weights[0:taps, :]
     second = weights[taps:, :]
     spans = [slice(2 * item * LANES, 2 * (item + 1) * LANES) for item in range(items)]
     branches, gradients, errors = {}, {}, []
 
-    def forward(item):
-        pre_act = jnp.dot(stacked[spans[item], :], first, preferred_element_type=F32)
-        sigmoid = jax.nn.sigmoid(pre_act)
+    def forward(part):
+        rows = stacked.shape[0] // 2
+        at = slice(part * rows, (part + 1) * rows)
+        pre_act = jnp.dot(stacked[at, :], first, preferred_element_type=F32)
+        sigmoid = 0.5 * jnp.tanh(0.5 * pre_act) + 0.5
         hidden = (pre_act * sigmoid).astype(BF)
-        hiddens[spans[item], :] = hidden
-        slopes[spans[item], :] = sigmoid * (1.0 + pre_act * (1.0 - sigmoid))
-        branches[item] = lax.dot_general(hidden, second, NT, preferred_element_type=F32).astype(BF)
+        hiddens[at, :] = hidden
+        slopes[at, :] = sigmoid * (1.0 + pre_act * (1.0 - sigmoid))
+        branch = lax.dot_general(hidden, second, NT, preferred_element_type=F32).astype(BF)
+        for n in range(items // 2):
+            branches[part * (items // 2) + n] = branch[2 * n * LANES : 2 * (n + 1) * LANES]
 
     def compare(item):
         branch, base, target = branches[item], fields[item].astype(F32), fields[items + item].astype(F32)
-        d_one = base + spectral(branch[:LANES]) - target
-        d_two = base + spectral(branch[LANES:]) - target
+        tendency = spectral(branch[:LANES], branch[LANES:])
+        d_one = base + tendency[0] - target
+        d_two = base + tendency[1] - target
         errors.append(0.375 * (d_one * d_one + d_two * d_two) + 0.25 * d_one * d_two)
         g_one = (cell_scale * (0.75 * d_one + 0.25 * d_two)).astype(BF)
         g_two = (cell_scale * (0.75 * d_two + 0.25 * d_one)).astype(BF)
-        gradients[item] = jnp.concatenate([spectral(g_one), spectral(g_two)], axis=0).astype(BF)
-
-    def backward(item):
-        g_hidden = jnp.dot(gradients[item], second, preferred_element_type=F32)
-        g_pres[spans[item], :] = (g_hidden * slopes[spans[item], :]).astype(BF)
-
-    stages = (forward, compare, backward)
-    for turn in range(items + len(stages) - 1):
-        for late, stage in enumerate(stages):
-            if 0 <= turn - late < items:
-                stage(turn - late)
+        gradients[item] = jnp.concatenate(spectral(g_one, g_two), axis=0).astype(BF)
+
+    def backward(part):
+        rows = stacked.shape[0] // 2
+        at = slice(part * rows, (part + 1) * rows)
+        count = items // 2
+        g_branch = jnp.concatenate([gradients[n] for n in range(part * count, (part + 1) * count)], axis=0)
+        g_hidden = jnp.dot(g_branch, second, preferred_element_type=F32)
+        g_pres[at, :] = (g_hidden * slopes[at, :]).astype(BF)
+
+    for part in range(2):
+        forward(part)
+    for item in range(items):
+        compare(item)
+    for part in range(2):
+        backward(part)
     loss = sum(errors[1:], errors[0])
     grads[0:taps, :] = lax.dot_general(stacked[...], g_pres[...], TN, preferred_element_type=F32)
     g_branch = jnp.concatenate([gradients[item] for item in range(items)], axis=0)

time: 44.9 us -> 43.9 us (0.978)
  Pallas kernels: 7.11 us -> 6.08 us
    pallas_call x1, Pallas kernels: 2.93 us -> 2.13 us  [kernel_body(): pl.pallas_call(functools.partial(step_kernel, items=items, k_in=k_in, k_o...]
where the time goes in v5:
time: 43.9 us; the launch traced here: 43.6 us
  blocking collectives  34.7 us (79%)
  Pallas kernels  6.08 us (14%)
  waiting for transfers between devices  1.73 us (4%)
  between operations  0.75 us (2%)
    all_to_all x1, blocking collectives, kernel_body(): lax.all_to_all(send, EVERY, 0, 0, tiled=True)  23 us
    all_to_all x1, blocking collectives, kernel_body(): back = lax.all_to_all(back, EVERY, 0, 0, tiled=True)  11.7 us
    pallas_call x1, Pallas kernels, kernel_body(): pl.pallas_call(pack_kernel, out_shape=shape(devices, rows, LANES, kind=BF...  2.32 us
    pallas_call x1, Pallas kernels, kernel_body(): pl.pallas_call(functools.partial(step_kernel, items=items, k_in=k_in, k_o...  2.13 us
    ppermute x1, waiting for transfers between devices, kernel_body(): came = lax.ppermute(give, 'lev', partners)  1.2 us
  transfers between devices with their start and end apart: 2, of which 2 were waited for; matrix products, arithmetic and copies ran while one was open for 0% of the time, Pallas kernels for 2%

profile of v5, /device:TPU:0, one launch (start us, length us, event | category | flops | bytes accessed | tf_op | source)
XLA Modules:
  0.0 43.6 jit_solution(8975323590934368305)
XLA Ops:
  0.6 2.3 %pack.1 = bf16[32,64,128]{2,1,0:T(8,128)(2,1)} custom-call(bf16[256,256]{1,0:T(8,128)(2,1)} %bitcast.20, bf16[256,256]{1,0:T(8,128)(2,1)} %bitcast.21, f32[128,256]{1,0:T(8,128)} %bitcast.22, s32[2,256]{1,0:T(2,128)} %refs_3_.1, f32[2,86]{1,0:T(2,128)} %refs_4_.1, f32[1,86]{1,0:T(1,128)} %bitcast.23, f32[48,64]{1,0:T(8,128)} %w_in.1, f32[16,64]{1,0:T(8,128)} %bitcast.16), custom_call_target="tpu_custom_call" | custom-call | tf_op jit(solution)/shard_map/pack/pallas_call | solution.py:473
  3.0 23.0 %all_to_all.10 = bf16[32,64,128]{2,1,0:T(8,128)(2,1)S(1)} all-to-all(bf16[32,64,128]{2,1,0:T(8,128)(2,1)} %pack.1), channel_id=1, replica_groups=mesh['lat'=8,'lev'=4] {'lat','lev'}, dimensions={0} | all-to-all | bytes 1048576 | tf_op jit(solution)/shard_map/all_to_all | solution.py:484
  25.9 0.1 collective-permute-start
  26.0 0.8 %prepare.1 = (bf16[1024,384]{1,0:T(8,128)(2,1)S(1)}, bf16[8,128,128]{2,1,0:T(8,128)(2,1)S(1)}, bf16[128,256]{1,0:T(8,128)(2,1)S(1)}, f32[128,128]{1,0:T(8,128)S(1)}, bf16[512,128]{1,0:T(8,128)(2,1)S(1)}) custom-call(bf16[8,4,64,128]{3,2,1,0:T(8,128)(2,1)S(1)} %bitcast.14), custom_call_target="tpu_custom_call" | custom-call | flops 4194304 | bytes 4194304 | tf_op jit(solution)/shard_map/prepare/pallas_call | solution.py:487
  26.8 0.5 %collective-permute-done.other = bf16[8,4,16,128]{3,2,1,0:T(8,128)(2,1)S(1)} collective-permute-done((bf16[8,4,16,128]{3,2,1,0:T(8,128)(2,1)S(1)}, bf16[8,4,16,128]{3,2,1,0:T(8,128)(2,1)S(1)}, u32[]{:S(2)}, u32[]{:S(2)}) %collective-permute-start) | collective-permute-done | bytes 131104 | tf_op jit(solution)/shard_map/ppermute | solution.py:486
  27.4 2.1 %step.1 = (bf16[8,4,16,128]{3,2,1,0:T(8,128)(2,1)S(1)}, f32[8,4,16,128]{3,2,1,0:T(8,128)S(1)}, bf16[8,128]{1,0:T(8,128)(2,1)S(1)}) custom-call(bf16[8,4,16,128]{3,2,1,0:T(8,128)(2,1)S(1)} %collective-permute-done.other, bf16[1024,384]{1,0:T(8,128)(2,1)S(1)} %get-tuple-element.22.stacked, bf16[8,128,128]{2,1,0:T(8,128)(2,1)S(1)} %get-tuple-element.23.fields, ...), custom_call_target="tpu_custom_call" | custom-call | tf_op jit(solution)/shard_map/step/pallas_call | solution.py:502
  29.5 0.2 collective-permute-start.1
  29.7 1.2 %collective-permute-done.1.came = bf16[8,4,16,128]{3,2,1,0:T(8,128)(2,1)S(1)} collective-permute-done((bf16[8,4,16,128]{3,2,1,0:T(8,128)(2,1)S(1)}, bf16[8,4,16,128]{3,2,1,0:T(8,128)(2,1)S(1)}, u32[]{:S(2)}, u32[]{:S(2)}) %collective-permute-start.1) | collective-permute-done | bytes 131104 | tf_op jit(solution)/shard_map/ppermute | solution.py:515
  30.9 0.0 copy-start
  30.9 0.0 copy-start.1
  31.0 0.0 copy-start.2
  31.0 0.0 copy-start.3
  31.0 0.0 copy-start.4
  31.0 0.0 copy-start.5
  31.0 11.7 %all_to_all.11 = bf16[32,24,128]{2,1,0:T(8,128)(2,1)S(1)} all-to-all(bf16[32,24,128]{2,1,0:T(8,128)(2,1)S(1)} %join.1), channel_id=1, replica_groups=mesh['lat'=8,'lev'=4] {'lat','lev'}, dimensions={0} | all-to-all | bytes 393216 | tf_op jit(solution)/shard_map/all_to_all | solution.py:522
  42.7 0.0 copy-done
  42.7 0.0 copy-done.1
  42.7 0.0 copy-done.2
  42.8 0.0 copy-done.3
  42.8 0.0 copy-done.4
  42.8 0.0 copy-done.5
  42.8 0.8 %update.1 = (f32[1,1]{1,0:T(1,128)}, f32[48,64]{1,0:T(8,128)}, f32[48,64]{1,0:T(8,128)}, f32[48,64]{1,0:T(8,128)}, f32[16,64]{1,0:T(8,128)}, /*index=5*/f32[16,64]{1,0:T(8,128)}, f32[16,64]{1,0:T(8,128)}) custom-call(bf16[16,2,24,128]{3,2,1,0:T(8,128)(2,1)S(1)} %bitcast.15, f32[48,64]{1,0:T(8,128)S(1)} %copy-done, f32[48,64]{1,0:T(8,128)S(1)} %copy-done.2, ...), custom_call_target="tpu_custom_call" | custom-call | tf_op jit(solution)/shard_map/update/pallas_call | solution.py:524
  (2 shorter events, 0.0 us)
Async XLA Ops:
  25.9 1.4 %collective-permute-start = (bf16[8,4,16,128]{3,2,1,0:T(8,128)(2,1)S(1)}, bf16[8,4,16,128]{3,2,1,0:T(8,128)(2,1)S(1)}, u32[]{:S(2)}, u32[]{:S(2)}) collective-permute-start(bf16[8,4,16,128]{3,2,1,0:T(8,128)(2,1)S(1)} %slice.4), channel_id=1, source_target_pairs={{0,1},{1,0},{2,3},{3,2},{4,5},{5,4},{6,7},{7,6},{8,9},{9,8},{10,11... | collective-permute-start | bytes 393224 | tf_op jit(solution)/shard_map/ppermute | solution.py:486
  29.5 1.4 %collective-permute-start.1 = (bf16[8,4,16,128]{3,2,1,0:T(8,128)(2,1)S(1)}, bf16[8,4,16,128]{3,2,1,0:T(8,128)(2,1)S(1)}, u32[]{:S(2)}, u32[]{:S(2)}) collective-permute-start(bf16[8,4,16,128]{3,2,1,0:T(8,128)(2,1)S(1)} %get-tuple-element.28), channel_id=1, source_target_pairs={{0,1},{1,0},{2,3},{3,2},{4,5},{5,4},{6,7},{7,6},{8,9},{9,8},{10,11... | collective-permute-start | bytes 393224 | tf_op jit(solution)/shard_map/ppermute | solution.py:515
  30.9 11.8 %copy-start = (f32[48,64]{1,0:T(8,128)S(1)}, f32[48,64]{1,0:T(8,128)}, u32[]{:S(2)}) copy-start(f32[48,64]{1,0:T(8,128)} %w_in.1) | copy-start | bytes 36868
  30.9 11.8 %copy-start.1 = (f32[64,16]{0,1:T(8,128)S(1)}, f32[64,16]{0,1:T(8,128)}, u32[]{:S(2)}) copy-start(f32[64,16]{0,1:T(8,128)} %param.19) | copy-start | bytes 12292
  31.0 11.8 %copy-start.2 = (f32[48,64]{1,0:T(8,128)S(1)}, f32[48,64]{1,0:T(8,128)}, u32[]{:S(2)}) copy-start(f32[48,64]{1,0:T(8,128)} %m_in.1) | copy-start | bytes 36868
  31.0 11.8 %copy-start.3 = (f32[48,64]{1,0:T(8,128)S(1)}, f32[48,64]{1,0:T(8,128)}, u32[]{:S(2)}) copy-start(f32[48,64]{1,0:T(8,128)} %v_in.1) | copy-start | bytes 36868
  31.0 11.8 %copy-start.4 = (f32[64,16]{0,1:T(8,128)S(1)}, f32[64,16]{0,1:T(8,128)}, u32[]{:S(2)}) copy-start(f32[64,16]{0,1:T(8,128)} %param.22) | copy-start | bytes 12292
  31.0 11.8 %copy-start.5 = (f32[64,16]{0,1:T(8,128)S(1)}, f32[64,16]{0,1:T(8,128)}, u32[]{:S(2)}) copy-start(f32[64,16]{0,1:T(8,128)} %param.23) | copy-start | bytes 12292

commit v6 on v5

--- a/solution.py
+++ b/solution.py
@@ -15,7 +15,8 @@
 BETA_TWO = 0.95
 EPSILON = 1e-08
 WEIGHT_DECAY = 0.1
-EVERY = ("lat", "lev")
+LAT, LEV = ("far", "near"), ("side", "core")
+EVERY = LAT + LEV
 BF = jnp.bfloat16
 F32 = jnp.float32
 
@@ -67,7 +68,7 @@
 ):
     items, rows, feats, lons = column_state.shape
     members = member_noise.shape[0]
-    lats, levs = lax.axis_size("lat"), lax.axis_size("lev")
+    lats, levs = lax.axis_size(LAT), lax.axis_size(LEV)
     devices = lats * levs
     lat_total, all_feats, own = lats * rows, levs * feats, lons // devices
     modes = legendre_basis.shape[1]
@@ -237,7 +238,7 @@
         for h in range(2)
     ]
     folded = jnp.stack(folded).astype(BF)
-    pairs = jnp.broadcast_to(folded[None], (devices // 2,) + folded.shape)
+    pairs = jnp.broadcast_to(folded[None, :, None], (2, 2, devices // 4) + folded.shape[1:])
     send[:, start : start + quarter, :] = pairs.reshape(devices, quarter, LANES)
     start += quarter
 
@@ -264,6 +265,19 @@
         send[g * share : (g + 1) * share, start:, :] = jnp.broadcast_to(block[None], (share, SUBLANES, LANES))
 
 
+def place(lat, lev, far):
+    return ((lat % 2 * 2 + lev % 2) * 2 + lev // 2) * far + lat // 2
+
+
+def back_place(lat, lev, far):
+    return ((lat % 2 * 2 + lev % 2) * far + lat // 2) * 2 + lev // 2
+
+
+def of_lev(got, lev, at):
+    lats = got.shape[0] // 4
+    return jnp.concatenate([got[place(lat, lev, lats // 2), at, :].astype(F32) for lat in range(lats)], axis=0)
+
+
 def row_starts(lats, k_in, k_out, quarter):
     return [
         [lat * k_in + q * quarter for q in range(k_in // quarter)]
@@ -272,43 +286,61 @@
     ]
 
 
-def unfold(half, weights, starts):
-    lats, levs, quarter, _ = half.shape
-    parts = quarters([half[:, lev].astype(F32).reshape(lats * quarter, LANES) for lev in range(levs)])
-    for q, part in enumerate(parts):
-        for lat in range(lats):
+def unfold(half, at, weights, starts):
+    quarter = at.stop - at.start
+    for q, part in enumerate(quarters([of_lev(half, lev, at) for lev in range(4)])):
+        for lat in range(len(starts)):
             at = starts[lat][q]
             weights[at : at + quarter, 0:LANES] = part[lat * quarter : (lat + 1) * quarter].astype(BF)
 
 
-def prepare_kernel(got, stacked, fields, operators, scales, weights, *, items, k_in, k_out, lons, modes):
-    lats, levs = got.shape[0], got.shape[1]
-    at_aux = got.shape[2] - SUBLANES
+def forward(stacked, weights, taps, at, hiddens, slopes, branches):
+    pre_act = jnp.dot(stacked[at, :], weights[0:taps, :], preferred_element_type=F32)
+    sigmoid = 0.5 * jnp.tanh(0.5 * pre_act) + 0.5
+    hidden = (pre_act * sigmoid).astype(BF)
+    hiddens[at, :] = hidden
+    slopes[at, :] = sigmoid * (1.0 + pre_act * (1.0 - sigmoid))
+    share = lax.dot_general(hidden, weights[taps:, :], NT, preferred_element_type=F32)
+    if branches is None:
+        return share
+    branches[at, :] = share
+
+
+def fold_gradients(stacked, g_pres, g_branch, hiddens, taps, starts, quarter, grads, out):
+    lats, levs = out.shape[0], out.shape[1]
+    grads[0:taps, :] = lax.dot_general(stacked, g_pres, TN, preferred_element_type=F32)
+    grads[taps:, :] = lax.dot_general(g_branch, hiddens, TN, preferred_element_type=F32)
+    parts = [jnp.concatenate([grads[s[q] : s[q] + quarter, :] for s in starts], axis=0) for q in range(4)]
+    for lev, part in enumerate(quarters(parts)):
+        out[:, lev] = part.reshape(lats, quarter, LANES).astype(out.dtype)
+
+
+def prepare_kernel(got, stacked, fields, operators, scales, weights, hiddens, slopes, branches, *, items, k_in, k_out, lons, modes):
+    lats, levs = got.shape[0] // 4, 4
+    at_aux = got.shape[1] - SUBLANES
     block = (LANES, LANES)
     lat_total = LANES // SUBLANES
     lane, row = lane_index(block), row_index(block)
 
     quarter = (k_in + k_out) // 4
-    own_half = got[:, :, at_aux - quarter : at_aux, :]
-    unfold(own_half, weights, row_starts(lats, k_in, k_out, quarter))
+    unfold(got, slice(at_aux - quarter, at_aux), weights, row_starts(lats, k_in, k_out, quarter))
 
     sums = []
     for lev in range(levs):
-        total = got[0, lev, at_aux:, :].astype(F32)
-        for lat in range(1, lats):
-            total = total + got[lat, lev, at_aux:, :].astype(F32)
-        sums.append(total)
+        total = of_lev(got, lev, slice(at_aux, at_aux + SUBLANES))
+        sums.append(jnp.sum(total.reshape(lats, SUBLANES, LANES), axis=0))
     sums = [s[6:7] for s in quarters(sums)]
     scale = [lax.rsqrt((sums[2 * m] + sums[2 * m + 1]) / (lat_total * lons) + 1e-05) for m in range(2)]
 
     def spread(rows):
         return jnp.concatenate([jnp.broadcast_to(r, (SUBLANES, LANES)) for r in rows], axis=0)
 
-    tops = [got[lat, 0, at_aux:, :].astype(F32) for lat in range(lats)]
+    tops = [got[place(lat, 0, lats // 2), at_aux:, :].astype(F32) for lat in range(lats)]
     high = spread([t[n : n + 1] for t in tops for n in range(2)])
     low = spread([t[n : n + 1] for t in tops for n in range(2, 4)])
     mask_rows = spread([t[n : n + 1] for t in tops for n in range(4, 6)])
-    device = lax.axis_index("lat") * levs + lax.axis_index("lev")
+    lat = lax.axis_index("far") * 2 + lax.axis_index("near")
+    device = place(lat, lax.axis_index("side") * 2 + lax.axis_index("core"), lats // 2)
     own = lane == device % lat_total * SUBLANES + row % SUBLANES
     mask = jnp.dot(jnp.where(own, mask_rows, 0.0).astype(BF), jnp.ones(block, BF), preferred_element_type=F32)
     latitude = row_index((lat_total, LANES)).astype(F32)
@@ -319,7 +351,7 @@
 
     def field_pair(group):
         at = slice(group * SUBLANES, (group + 1) * SUBLANES)
-        parts = quarters([got[:, lev, at, :].astype(F32).reshape(lats * SUBLANES, LANES) for lev in range(levs)])
+        parts = quarters([of_lev(got, lev, at) for lev in range(levs)])
         parts = [q.reshape(lats, 1, SUBLANES, LANES) for q in parts]
         return [jnp.concatenate(parts[2 * k : 2 * k + 2], axis=1).reshape(block) for k in range(2)]
 
@@ -343,16 +375,20 @@
     high = operator.astype(BF)
     operators[...] = jnp.concatenate([high, (operator - high.astype(F32)).astype(BF)], axis=1)
 
+    taps = lats * k_in
+    for part in range(2):
+        at = slice(part * items * LANES, (part + 1) * items * LANES)
+        forward(stacked, weights, taps, at, hiddens, slopes, branches)
+
 
 def step_kernel(
-    other, stacked, fields, operators, scales, own, give, keep, losses, weights, hiddens, slopes, g_pres, grads, *, items, k_in, k_out
+    other, stacked, fields, operators, scales, own_branches, give, losses, g_branches, weights, hiddens, slopes, g_pres, grads,
+    *, items, k_in, k_out
 ):
-    lats, levs, quarter, _ = other.shape
+    lats, quarter = other.shape[0] // 4, other.shape[1]
     taps = lats * k_in
     starts = row_starts(lats, k_in, k_out, quarter)
-    unfold(other[...], weights, starts)
-    weights[:, LANES:] = own[...]
-
+    unfold(other, slice(0, quarter), weights, starts)
     operator, cell_scale = operators[...], scales[...]
 
     def spectral(one, two):
@@ -360,24 +396,19 @@
         out = jnp.dot(operator, jnp.concatenate([v, v], axis=0), preferred_element_type=F32)
         return out[:, :LANES], out[:, LANES:]
 
-    first = weights[0:taps, :]
-    second = weights[taps:, :]
-    spans = [slice(2 * item * LANES, 2 * (item + 1) * LANES) for item in range(items)]
     branches, gradients, errors = {}, {}, []
-
-    def forward(part):
-        rows = stacked.shape[0] // 2
-        at = slice(part * rows, (part + 1) * rows)
-        pre_act = jnp.dot(stacked[at, :], first, preferred_element_type=F32)
-        sigmoid = 0.5 * jnp.tanh(0.5 * pre_act) + 0.5
-        hidden = (pre_act * sigmoid).astype(BF)
-        hiddens[at, :] = hidden
-        slopes[at, :] = sigmoid * (1.0 + pre_act * (1.0 - sigmoid))
-        branch = lax.dot_general(hidden, second, NT, preferred_element_type=F32).astype(BF)
-        for n in range(items // 2):
-            branches[part * (items // 2) + n] = branch[2 * n * LANES : 2 * (n + 1) * LANES]
-
-    def compare(item):
+    halves_of_items = [range(part * items // 2, (part + 1) * items // 2) for part in range(2)]
+
+    def cells_of(chosen):
+        return slice(2 * chosen[0] * LANES, 2 * (chosen[-1] + 1) * LANES)
+
+    for chosen in halves_of_items:
+        at = cells_of(chosen)
+        branch = (own_branches[at, :] + forward(stacked, weights, taps, at, hiddens, slopes, None)).astype(BF)
+        for place, item in enumerate(chosen):
+            branches[item] = branch[2 * place * LANES : 2 * (place + 1) * LANES]
+
+    for item in range(items):
         branch, base, target = branches[item], fields[item].astype(F32), fields[items + item].astype(F32)
         tendency = spectral(branch[:LANES], branch[LANES:])
         d_one = base + tendency[0] - target
@@ -387,25 +418,15 @@
         g_two = (cell_scale * (0.75 * d_two + 0.25 * d_one)).astype(BF)
         gradients[item] = jnp.concatenate(spectral(g_one, g_two), axis=0).astype(BF)
 
-    def backward(part):
-        rows = stacked.shape[0] // 2
-        at = slice(part * rows, (part + 1) * rows)
-        count = items // 2
-        g_branch = jnp.concatenate([gradients[n] for n in range(part * count, (part + 1) * count)], axis=0)
-        g_hidden = jnp.dot(g_branch, second, preferred_element_type=F32)
+    for chosen in halves_of_items:
+        at = cells_of(chosen)
+        g_branch = jnp.concatenate([gradients[item] for item in chosen], axis=0)
+        g_branches[at, :] = g_branch
+        g_hidden = jnp.dot(g_branch, weights[taps:, :], preferred_element_type=F32)
         g_pres[at, :] = (g_hidden * slopes[at, :]).astype(BF)
-
-    for part in range(2):
-        forward(part)
-    for item in range(items):
-        compare(item)
-    for part in range(2):
-        backward(part)
+    fold_gradients(stacked[...], g_pres[...], g_branches[...], hiddens[...], taps, starts, quarter, grads, give)
+
     loss = sum(errors[1:], errors[0])
-    grads[0:taps, :] = lax.dot_general(stacked[...], g_pres[...], TN, preferred_element_type=F32)
-    g_branch = jnp.concatenate([gradients[item] for item in range(items)], axis=0)
-    grads[taps:, :] = lax.dot_general(g_branch, hiddens[...], TN, preferred_element_type=F32)
-
     loss_part = jnp.sum(loss * cell_scale, keepdims=True)
     terms = []
     for _ in range(3):
@@ -414,24 +435,30 @@
         loss_part = loss_part - term
     terms.append(jnp.zeros((SUBLANES - 3, LANES), F32))
     losses[...] = jnp.concatenate(terms, axis=0).astype(BF)
-    for p, half in enumerate((give, keep)):
-        columns = slice(p * LANES, (p + 1) * LANES)
-        parts = [
-            jnp.concatenate([grads[s[q] : s[q] + quarter, columns] for s in starts], axis=0) for q in range(4)
-        ]
-        for lev, part in enumerate(quarters(parts)):
-            half[:, lev] = part.reshape(lats, quarter, LANES).astype(half.dtype)
+
+
+def keep_kernel(stacked, own, hiddens, slopes, g_branches, keep, g_pres, grads, *, k_in, k_out):
+    lats, quarter = keep.shape[0], keep.shape[2]
+    taps, cells = lats * k_in, stacked.shape[0]
+    for part in range(2):
+        at = slice(part * cells // 2, (part + 1) * cells // 2)
+        g_hidden = jnp.dot(g_branches[at, :], own[taps:, :], preferred_element_type=F32)
+        g_pres[at, :] = (g_hidden * slopes[at, :]).astype(BF)
+    starts = row_starts(lats, k_in, k_out, quarter)
+    fold_gradients(stacked[...], g_pres[...], g_branches[...], hiddens[...], taps, starts, quarter, grads, keep)
 
 
 def join_kernel(keep, came, losses, send):
-    quarter = keep.shape[2]
+    lats, levs, quarter, _ = keep.shape
     total = (keep[...] + came[...].astype(F32)).astype(BF)
-    send[:, :quarter, :] = total.reshape(-1, quarter, LANES)
+    for lat in range(lats):
+        for lev in range(levs):
+            send[back_place(lat, lev, lats // 2), :quarter, :] = total[lat, lev]
     send[:, quarter:, :] = jnp.broadcast_to(losses[...][None], (send.shape[0], SUBLANES, LANES))
 
 
 def update_kernel(got, w_in, m_in, v_in, w_out, m_out, v_out, loss, nw_in, nm_in, nv_in, nw_out, nm_out, nv_out):
-    total = jnp.sum(got[...].astype(F32), axis=0)
+    total = jnp.sum(jnp.sum(got[...].astype(F32), axis=2), axis=0)
     at_loss = total.shape[1] - SUBLANES
 
     def unfolded(rows):
@@ -446,14 +473,14 @@
 
 def kernel_body(state, target, noise, mask, basis, mode_filter, w_in, w_out, m_in, v_in, m_out, v_out):
     items, _, _, lons = state.shape
-    lats, levs = lax.axis_size("lat"), lax.axis_size("lev")
-    devices = lats * levs
+    far, levs = lax.axis_size("far"), 4
+    lats, devices = 2 * far, 8 * far
     k_in, k_out, modes = w_in.shape[0], w_out.shape[1], basis.shape[1]
     quarter = (k_in + k_out) // 4
     at_weights = SUBLANES * (items + 1)
     rows = at_weights + quarter + SUBLANES
     inputs, cells = lats * (k_in + k_out), 2 * items * LANES
-    partners = [(i, i ^ 1) for i in range(levs)]
+    partners = [(0, 1), (1, 0)]
     vmem, hbm = pl.BlockSpec(memory_space=pltpu.VMEM), pl.BlockSpec(memory_space=pltpu.HBM)
     small = pltpu.CompilerParams(vmem_limit_bytes=8 * 2**20)
 
@@ -481,10 +508,9 @@
         ],
         name="pack",
     )(*sources)
-    got = lax.all_to_all(send, EVERY, 0, 0, tiled=True).reshape(lats, levs, rows, LANES)
-    own = got[:, :, at_weights : at_weights + quarter]
-    other = lax.ppermute(own, "lev", partners)
-    prepared = pl.pallas_call(
+    got = lax.all_to_all(send, ("near", "core", "side", "far"), 0, 0, tiled=True)
+    other = lax.ppermute(got[:, at_weights : at_weights + quarter], "core", partners)
+    stacked, fields, operators, scales, own, hiddens, slopes, branches = pl.pallas_call(
         functools.partial(prepare_kernel, items=items, k_in=k_in, k_out=k_out, lons=lons, modes=modes),
         out_shape=(
             shape(cells, 3 * LANES, kind=BF),
@@ -492,48 +518,61 @@
             shape(LANES, 2 * LANES, kind=BF),
             shape(LANES, LANES),
             shape(inputs, LANES, kind=BF),
+            shape(cells, LANES, kind=BF),
+            shape(cells, LANES),
+            shape(cells, LANES),
         ),
         in_specs=[vmem],
         compiler_params=small,
-        cost_estimate=pl.CostEstimate(flops=2**22, bytes_accessed=2**22, transcendentals=0),
+        cost_estimate=pl.CostEstimate(flops=2**28, bytes_accessed=2**22, transcendentals=0),
         name="prepare",
     )(got)
     block = (lats, levs, quarter, LANES)
-    give, keep, losses = pl.pallas_call(
+    give, losses, g_branches = pl.pallas_call(
         functools.partial(step_kernel, items=items, k_in=k_in, k_out=k_out),
-        out_shape=(shape(*block, kind=BF), shape(*block), shape(SUBLANES, LANES, kind=BF)),
+        out_shape=(shape(*block, kind=BF), shape(SUBLANES, LANES, kind=BF), shape(cells, LANES, kind=BF)),
         scratch_shapes=[
-            pltpu.VMEM((inputs, 2 * LANES), BF),
-            pltpu.VMEM((cells, 2 * LANES), BF),
-            pltpu.VMEM((cells, 2 * LANES), F32),
-            pltpu.VMEM((cells, 2 * LANES), BF),
-            pltpu.VMEM((inputs, 2 * LANES), F32),
+            pltpu.VMEM((inputs, LANES), BF),
+            pltpu.VMEM((cells, LANES), BF),
+            pltpu.VMEM((cells, LANES), F32),
+            pltpu.VMEM((cells, LANES), BF),
+            pltpu.VMEM((inputs, LANES), F32),
         ],
         compiler_params=pltpu.CompilerParams(vmem_limit_bytes=16 * 2**20),
         name="step",
-    )(other, *prepared)
-    came = lax.ppermute(give, "lev", partners)
+    )(other, stacked, fields, operators, scales, branches)
+    came = lax.ppermute(give, "core", partners)
+    keep = pl.pallas_call(
+        functools.partial(keep_kernel, k_in=k_in, k_out=k_out),
+        out_shape=shape(*block),
+        scratch_shapes=[pltpu.VMEM((cells, LANES), BF), pltpu.VMEM((inputs, LANES), F32)],
+        compiler_params=small,
+        cost_estimate=pl.CostEstimate(flops=2**28, bytes_accessed=2**22, transcendentals=0),
+        name="keep",
+    )(stacked, own, hiddens, slopes, g_branches)
     back = pl.pallas_call(
         join_kernel,
         out_shape=shape(devices, quarter + SUBLANES, LANES, kind=BF),
         compiler_params=small,
         name="join",
     )(keep, came, losses)
-    back = lax.all_to_all(back, EVERY, 0, 0, tiled=True)
+    back = lax.all_to_all(back, ("near", "core", "far", "side"), 0, 0, tiled=True)
     wide, tall = shape(*w_in.shape), shape(*w_out.shape[::-1])
     loss, *new = pl.pallas_call(
         update_kernel,
         out_shape=(shape(1, 1), wide, wide, wide, tall, tall, tall),
         compiler_params=small,
         name="update",
-    )(back.reshape(-1, 2, quarter + SUBLANES, LANES), w_in, m_in, v_in, w_out.T, m_out.T, v_out.T)
+    )(back.reshape(2, 2, devices // 4, quarter + SUBLANES, LANES), w_in, m_in, v_in, w_out.T, m_out.T, v_out.T)
     return (loss.reshape(()), *new[:3], *[n.T for n in new[3:]])
 
 
 def solution(mesh):
-    field = P(None, "lat", "lev", None)
-    row, first, second = P("lat", None), P("lat", "lev"), P("lev", "lat")
     lats, levs = mesh.shape["lat"], mesh.shape["lev"]
+    near, core = math.gcd(lats, 2), math.gcd(levs, 2)
+    finer = jax.sharding.Mesh(mesh.devices.reshape(lats // near, near, levs // core, core), EVERY)
+    field = P(None, LAT, LEV, None)
+    row, first, second = P(LAT, None), P(LAT, LEV), P(LEV, LAT)
 
     def body(*arrays):
         step = kernel_body if kernels_fit(arrays, lats, levs) else plain_body
@@ -541,7 +580,7 @@
 
     return jax.shard_map(
         body,
-        mesh=mesh,
+        mesh=finer,
         in_specs=(field, field, field, row, row, P(), first, second, first, first, second, second),
         out_specs=(P(), first, first, first, second, second, second),
         check_vma=False,

time: 43.9 us -> 42.4 us (0.966)
  waiting for transfers between devices: 1.73 us -> 0.32 us
  blocking collectives: 34.7 us -> 33.3 us
  Pallas kernels: 6.08 us -> 6.95 us
  starting transfers between devices: 0.28 us -> 0.76 us
    all_to_all x2, blocking collectives: 34.7 us -> 33.3 us  [the longest x1 23 us: kernel_body(): lax.all_to_all(send, ('near', 'core', 'side', 'far'), 0, 0, tiled=True)]
    ppermute x2, waiting for transfers between devices: 1.73 us -> 0.32 us  [the longest x1 0.31 us: kernel_body(): came = lax.ppermute(give, 'core', partners)]
    pallas_call x0 -> x1, Pallas kernels: none -> 0.8 us  [kernel_body(): pl.pallas_call(functools.partial(keep_kernel, k_in=k_in, k_out=k_out), ou...]
    ppermute x2, starting transfers between devices: 0.28 us -> 0.76 us  [the longest x1 0.47 us: kernel_body(): lax.ppermute(got[:, at_weights:at_weights + quarter], 'core', partners)]
  transfers between devices with their start and end apart: 2 -> 2, of which waited for: 2 -> 1; matrix products, arithmetic and copies ran while one was open for 0% -> 0% of each run, Pallas kernels for 2% -> 5%
where the time goes in v6:
time: 42.4 us; the launch traced here: 42.1 us
  blocking collectives  33.3 us (79%)
  Pallas kernels  6.95 us (16%)
  starting transfers between devices  0.76 us (2%)
  between operations  0.74 us (2%)
    all_to_all x1, blocking collectives, kernel_body(): lax.all_to_all(send, ('near', 'core', 'side', 'far'), 0, 0, tiled=True)  23 us
    all_to_all x1, blocking collectives, kernel_body(): lax.all_to_all(back, ('near', 'core', 'far', 'side'), 0, 0, tiled=True)  10.2 us
    pallas_call x1, Pallas kernels, kernel_body(): pl.pallas_call(pack_kernel, out_shape=shape(devices, rows, LANES, kind=BF...  2.32 us
    pallas_call x1, Pallas kernels, kernel_body(): pl.pallas_call(functools.partial(step_kernel, items=items, k_in=k_in, k_o...  1.88 us
    pallas_call x1, Pallas kernels, kernel_body(): pl.pallas_call(functools.partial(prepare_kernel, items=items, k_in=k_in,...  1.11 us
  transfers between devices with their start and end apart: 2, of which 1 were waited for; matrix products, arithmetic and copies ran while one was open for 0% of the time, Pallas kernels for 5%

profile of v6, /device:TPU:0, one launch (start us, length us, event | category | flops | bytes accessed | tf_op | source)
XLA Modules:
  0.0 42.1 jit_solution(2759393794634454751)
XLA Ops:
  0.6 2.3 %pack.1 = bf16[32,64,128]{2,1,0:T(8,128)(2,1)} custom-call(bf16[256,256]{1,0:T(8,128)(2,1)} %bitcast.17, bf16[256,256]{1,0:T(8,128)(2,1)} %bitcast.18, f32[128,256]{1,0:T(8,128)} %bitcast.19, s32[2,256]{1,0:T(2,128)} %refs_3_.1, f32[2,86]{1,0:T(2,128)} %refs_4_.1, f32[1,86]{1,0:T(1,128)} %bitcast.20, f32[48,64]{1,0:T(8,128)} %w_in.1, f32[16,64]{1,0:T(8,128)} %bitcast.13), custom_call_target="tpu_custom_call" | custom-call | tf_op jit(solution)/shard_map/pack/pallas_call | solution.py:500
  3.0 23.0 %all_to_all.10.got = bf16[32,64,128]{2,1,0:T(8,128)(2,1)S(1)} all-to-all(bf16[32,64,128]{2,1,0:T(8,128)(2,1)} %pack.1), channel_id=1, replica_groups=mesh['far'=4,'near'=2,'side'=2,'core'=2] {'near','core','side','far'}, dimensions={0} | all-to-all | bytes 1048576 | tf_op jit(solution)/shard_map/all_to_all | solution.py:511
  26.0 0.5 %collective-permute-start = (bf16[32,16,128]{2,1,0:T(8,128)(2,1)S(1)}, bf16[32,16,128]{2,1,0:T(8,128)(2,1)S(1)}, u32[]{:S(2)}, u32[]{:S(2)}) collective-permute-start(bf16[32,16,128]{2,1,0:T(8,128)(2,1)S(1)} %slice.4), channel_id=1, source_target_pairs={{0,1},{1,0},{2,3},{3,2},{4,5},{5,4},{6,7},{7,6},{8,9},{9,8},{10,11... | collective-permute-start | bytes 393224 | tf_op jit(solution)/shard_map/ppermute | solution.py:512
  26.5 1.1 %prepare.1 = (bf16[1024,384]{1,0:T(8,128)(2,1)S(1)}, bf16[8,128,128]{2,1,0:T(8,128)(2,1)S(1)}, bf16[128,256]{1,0:T(8,128)(2,1)S(1)}, f32[128,128]{1,0:T(8,128)S(...) custom-call(bf16[32,64,128]{2,1,0:T(8,128)(2,1)S(1)} %all_to_all.10.got), custom_call_target="tpu_custom_call" | custom-call | flops 268435456 | bytes 4194304 | tf_op jit(solution)/shard_map/prepare/pallas_call | solution.py:513
  27.6 0.0 collective-permute-done.other
  27.6 1.9 %step.1 = (bf16[8,4,16,128]{3,2,1,0:T(8,128)(2,1)S(1)}, bf16[8,128]{1,0:T(8,128)(2,1)S(1)}, bf16[1024,128]{1,0:T(8,128)(2,1)S(1)}) custom-call(bf16[32,16,128]{2,1,0:T(8,128)(2,1)S(1)} %collective-permute-done.other, bf16[1024,384]{1,0:T(8,128)(2,1)S(1)} %get-tuple-element.25.stacked, bf16[8,128,128]{2,1,0:T(8,128)(2,1)S(1)} %get-tuple-element.29.fields, ...), custom_call_target="tpu_custom_call" | custom-call | tf_op jit(solution)/shard_map/step/pallas_call | solution.py:531
  29.5 0.3 collective-permute-start.1
  29.8 0.8 %keep.1 = f32[8,4,16,128]{3,2,1,0:T(8,128)S(1)} custom-call(bf16[1024,384]{1,0:T(8,128)(2,1)S(1)} %get-tuple-element.25.stacked, bf16[512,128]{1,0:T(8,128)(2,1)S(1)} %get-tuple-element.26.own, bf16[1024,128]{1,0:T(8,128)(2,1)S(1)} %get-tuple-element.27.hiddens, f32[1024,128]{1,0:T(8,128)S(1)} %get-tuple-element.28.slopes, ...), custom_call_target="tpu_custom_call" | custom-call | flops 268435456 | bytes 4194304 | tf_op jit(solution)/shard_map/keep/pallas_call | solution.py:545
  30.6 0.3 collective-permute-done.1.came
  31.0 0.0 copy-start
  31.0 0.0 copy-start.1
  31.0 0.0 copy-start.2
  31.0 0.0 copy-start.3
  31.0 0.0 copy-start.4
  31.0 0.0 copy-start.5
  31.0 10.2 %all_to_all.11 = bf16[32,24,128]{2,1,0:T(8,128)(2,1)S(1)} all-to-all(bf16[32,24,128]{2,1,0:T(8,128)(2,1)S(1)} %join.1), channel_id=1, replica_groups=mesh['far'=4,'near'=2,'side'=2,'core'=2] {'near','core','far','side'}, dimensions={0} | all-to-all | bytes 393216 | tf_op jit(solution)/shard_map/all_to_all | solution.py:559
  41.2 0.0 copy-done
  41.2 0.0 copy-done.1
  41.2 0.0 copy-done.2
  41.2 0.0 copy-done.3
  41.3 0.0 copy-done.4
  41.3 0.0 copy-done.5
  41.3 0.8 %update.1 = (f32[1,1]{1,0:T(1,128)}, f32[48,64]{1,0:T(8,128)}, f32[48,64]{1,0:T(8,128)}, f32[48,64]{1,0:T(8,128)}, f32[16,64]{1,0:T(8,128)}, /*index=5*/f32[16,64]{1,0:T(8,128)}, f32[16,64]{1,0:T(8,128)}) custom-call(bf16[2,2,8,24,128]{4,3,2,1,0:T(8,128)(2,1)S(1)} %bitcast.12, f32[48,64]{1,0:T(8,128)S(1)} %copy-done, f32[48,64]{1,0:T(8,128)S(1)} %copy-done.2, ...), custom_call_target="tpu_custom_call" | custom-call | tf_op jit(solution)/shard_map/update/pallas_call | solution.py:561
  (2 shorter events, 0.1 us)
Async XLA Ops:
  26.0 1.6 %collective-permute-start = (bf16[32,16,128]{2,1,0:T(8,128)(2,1)S(1)}, bf16[32,16,128]{2,1,0:T(8,128)(2,1)S(1)}, u32[]{:S(2)}, u32[]{:S(2)}) collective-permute-start(bf16[32,16,128]{2,1,0:T(8,128)(2,1)S(1)} %slice.4), channel_id=1, source_target_pairs={{0,1},{1,0},{2,3},{3,2},{4,5},{5,4},{6,7},{7,6},{8,9},{9,8},{10,11... | collective-permute-start | bytes 393224 | tf_op jit(solution)/shard_map/ppermute | solution.py:512
  29.5 1.4 %collective-permute-start.1 = (bf16[8,4,16,128]{3,2,1,0:T(8,128)(2,1)S(1)}, bf16[8,4,16,128]{3,2,1,0:T(8,128)(2,1)S(1)}, u32[]{:S(2)}, u32[]{:S(2)}) collective-permute-start(bf16[8,4,16,128]{3,2,1,0:T(8,128)(2,1)S(1)} %get-tuple-element.34), channel_id=1, source_target_pairs={{0,1},{1,0},{2,3},{3,2},{4,5},{5,4},{6,7},{7,6},{8,9},{9,8},{10,11... | collective-permute-start | bytes 393224 | tf_op jit(solution)/shard_map/ppermute | solution.py:544
  31.0 10.3 %copy-start = (f32[48,64]{1,0:T(8,128)S(1)}, f32[48,64]{1,0:T(8,128)}, u32[]{:S(2)}) copy-start(f32[48,64]{1,0:T(8,128)} %w_in.1) | copy-start | bytes 36868
  31.0 10.3 %copy-start.1 = (f32[64,16]{0,1:T(8,128)S(1)}, f32[64,16]{0,1:T(8,128)}, u32[]{:S(2)}) copy-start(f32[64,16]{0,1:T(8,128)} %param.19) | copy-start | bytes 12292
  31.0 10.3 %copy-start.2 = (f32[48,64]{1,0:T(8,128)S(1)}, f32[48,64]{1,0:T(8,128)}, u32[]{:S(2)}) copy-start(f32[48,64]{1,0:T(8,128)} %m_in.1) | copy-start | bytes 36868
  31.0 10.3 %copy-start.3 = (f32[48,64]{1,0:T(8,128)S(1)}, f32[48,64]{1,0:T(8,128)}, u32[]{:S(2)}) copy-start(f32[48,64]{1,0:T(8,128)} %v_in.1) | copy-start | bytes 36868
  31.0 10.3 %copy-start.4 = (f32[64,16]{0,1:T(8,128)S(1)}, f32[64,16]{0,1:T(8,128)}, u32[]{:S(2)}) copy-start(f32[64,16]{0,1:T(8,128)} %param.22) | copy-start | bytes 12292
  31.0 10.3 %copy-start.5 = (f32[64,16]{0,1:T(8,128)S(1)}, f32[64,16]{0,1:T(8,128)}, u32[]{:S(2)}) copy-start(f32[64,16]{0,1:T(8,128)} %param.23) | copy-start | bytes 12292
